TPU v7x, 256 devices: a whole 4x4x8 slice. The times are simulated.
256 devices in a mesh: gz: 64 (over x, z, core), gy: 4 (over y).
Axes of the slice: x: 4, y: 4, z: 8, core: 2. Of those that a mesh axis runs over, the one named last changes fastest.
Arguments:
- populations: float32 [19, 64, 128, 256], P(None, 'gz', 'gy'), may hold values from 0 to 0.5, as said below
- solid_fraction: float32 [64, 128, 256], P('gz', 'gy'), may hold values from 0 to 1
- labels: int32 [64, 128, 256], P('gz', 'gy'), may hold values from 0 to 4, as said below
Outputs:
- sensitivity: float32 [64, 128, 256], P('gz', 'gy')
- adjoint_populations: float32 [19, 64, 128, 256], P(None, 'gz', 'gy')
Inputs may be any that keep to these rules, and one draw needn't show every extreme that they name: `populations`: each population is w_q times a factor between 0.7 and 1.3. labels 3 appear only in the first plane along the feeding direction and 4 only in the last, in voxels that are not solid.
All inputs are finite; a program needn't handle non-finite values.
Results may differ from a plain program's by a relative error of at most 0.00028.
Values sent between devices are 32-bit elements; how exact they have to be, the bound alone decides.
A program may use at most 64 MiB of HBM per device.

v0:
```python
import jax
import jax.numpy as jnp
from jax import lax
from jax.sharding import PartitionSpec as P

STEPS = 2


OMEGA = 0.9
INLET_SPEED = 0.05


def padded_2(cells, sides, width):
    for axis, dim in sides:
        count = lax.axis_size(axis)
        head = lax.slice_in_dim(cells, 0, width, axis=dim)
        tail = lax.slice_in_dim(cells, cells.shape[dim] - width, cells.shape[dim], axis=dim)
        cells = jnp.concatenate(
            [
                lax.ppermute(tail, axis, [(i, (i + 1) % count) for i in range(count)]),
                cells,
                lax.ppermute(head, axis, [((i + 1) % count, i) for i in range(count)]),
            ],
            axis=dim,
        )
    return cells


def velocity_table():
    velocities = [(0, 0, 0)]
    for axis in range(3):
        for sign in (1, -1):
            vector = [0, 0, 0]
            vector[axis] = sign
            velocities.append(tuple(vector))
    for first in range(3):
        for second in range(first + 1, 3):
            for sign_a in (1, -1):
                for sign_b in (1, -1):
                    vector = [0, 0, 0]
                    vector[first] = sign_a
                    vector[second] = sign_b
                    velocities.append(tuple(vector))
    weights = [1.0 / 3.0] + [1.0 / 18.0] * 6 + [1.0 / 36.0] * 12
    opposite = [velocities.index(tuple((-e for e in vector))) for vector in velocities]
    return (velocities, weights, opposite)


def equilibrium(density, vel_x, vel_y, vel_z):
    velocities, weights, opposite = velocity_table()
    rows = []
    speed = vel_x * vel_x + vel_y * vel_y + vel_z * vel_z
    for index in range(19):
        cx, cy, cz = velocities[index]
        along = cx * vel_x + cy * vel_y + cz * vel_z
        rows.append(
            weights[index] * density * (1.0 + 3.0 * along + 4.5 * along * along - 1.5 * speed)
        )
    return jnp.stack(rows)


def moments(field):
    velocities, weights, opposite = velocity_table()
    density = jnp.sum(field, axis=0)
    mom_x = sum((velocities[q][0] * field[q] for q in range(19) if velocities[q][0] != 0))
    mom_y = sum((velocities[q][1] * field[q] for q in range(19) if velocities[q][1] != 0))
    mom_z = sum((velocities[q][2] * field[q] for q in range(19) if velocities[q][2] != 0))
    return (density, mom_x, mom_y, mom_z)


def collide(field, s_eff, labels):
    velocities, weights, opposite = velocity_table()
    density, mom_x, mom_y, mom_z = moments(field)
    feq = equilibrium(density, mom_x / density, mom_y / density, mom_z / density)
    rate = jnp.where(labels == 4, jnp.float32(1.0), jnp.float32(OMEGA))
    relaxed = field - rate * (field - feq)
    flipped = jnp.stack([field[opposite[q]] for q in range(19)])
    mixed = (1.0 - s_eff) * relaxed + s_eff * flipped
    ones = jnp.ones_like(density)
    inlet = equilibrium(ones, 0.0 * ones, 0.0 * ones, INLET_SPEED * ones)
    return jnp.where(labels == 3, inlet, mixed)


def energy(field, s_eff):
    density, mom_x, mom_y, mom_z = moments(field)
    return jnp.sum((1.0 - s_eff) * (mom_x * mom_x + mom_y * mom_y + mom_z * mom_z) / density)


def stream(field, sense):
    velocities, weights, opposite = velocity_table()
    depth = field.shape[1]
    height = field.shape[2]
    offsets = [(sense * v[0], sense * v[1], sense * v[2]) for v in velocities]
    padded = padded_2(field, (("gz", 1), ("gy", 2)), 1)
    moved = [
        padded[
            q,
            1 - offsets[q][2] : 1 - offsets[q][2] + depth,
            1 - offsets[q][1] : 1 - offsets[q][1] + height,
            :,
        ]
        for q in range(19)
    ]
    return jnp.stack([jnp.roll(moved[q], offsets[q][0], axis=2) for q in range(19)])


def global_energy(value):
    return lax.psum(value, ("gz", "gy"))


def on_device(populations, solid_fraction, labels):
    s_eff = jnp.where(
        labels == 1, solid_fraction, jnp.where(labels == 2, jnp.float32(1.0), jnp.float32(0.0))
    )
    states = [populations]
    total = jnp.float32(0.0)
    for step in range(STEPS):
        nxt = stream(collide(states[-1], s_eff, labels), 1)
        states.append(nxt)
        total = total + global_energy(energy(nxt, s_eff))
    energy_grad = jax.grad(energy, argnums=(0, 1))
    adjoint = jnp.zeros_like(populations)
    fraction_grad = jnp.zeros_like(solid_fraction)
    for step in reversed(range(STEPS)):
        grad_field, grad_frac = energy_grad(states[step + 1], s_eff)
        adjoint = adjoint + grad_field
        fraction_grad = fraction_grad + grad_frac
        pulled = stream(adjoint, -1)
        unused, pullback = jax.vjp(
            lambda field, frac: collide(field, frac, labels), states[step], s_eff
        )
        adjoint, grad_frac = pullback(pulled)
        fraction_grad = fraction_grad + grad_frac
    cells = (
        populations.shape[1]
        * populations.shape[2]
        * populations.shape[3]
        * lax.axis_size("gz")
        * lax.axis_size("gy")
    )
    mean_energy = total / (STEPS * cells)
    sensitivity = jnp.where(labels == 1, fraction_grad, jnp.float32(0.0)) / mean_energy
    return (sensitivity, adjoint / mean_energy)


def solution(mesh):
    in_specs = (P(None, "gz", "gy", None), P("gz", "gy", None), P("gz", "gy", None))
    out_specs = (P("gz", "gy", None), P(None, "gz", "gy", None))
    return jax.shard_map(
        on_device, mesh=mesh, in_specs=in_specs, out_specs=out_specs, check_vma=False
    )
```

profile of v0, /device:TPU:1, one launch (start us, length us, event | category | flops | bytes accessed | tf_op | source)
XLA Modules:
  0.0 173.0 jit_solution(15628574961668883643)
XLA Ops:
  0.7 0.8 constant_dynamic-update-slice_fusion.50
  1.5 1.1 reduce_sum.1999
  2.6 0.7 constant_dynamic-update-slice_fusion.31
  4.1 0.7 copy-done.11
  5.1 0.2 add_select_fusion.1
  5.4 0.5 copy-done.7
  6.1 3.0 %collective-permute-start = (f32[19,1,32,256]{3,2,1,0:T(8,128)S(1)}, f32[19,1,32,256]{3,2,1,0:T(8,128)S(1)}, u32[]{:S(2)}, u32[]{:S(2)}) collective-permute-start(f32[19,1,32,256]{3,2,1,0:T(8,128)S(1)} %add_select_fusion.1), channel_id=1, source_target_pairs={{0,4},{4,8},{8,12},{12,16},{16,20},{20,24},{24,28},{28,32},{32,36}... | collective-permute-start | bytes 1867784 | tf_op jit(solution)/shard_map/ppermute | solution.py:20
  9.5 9.6 %collective-permute-done.1 = f32[19,1,32,256]{3,2,1,0:T(8,128)S(1)} collective-permute-done((f32[19,1,32,256]{3,2,1,0:T(8,128)S(1)}, f32[19,1,32,256]{3,2,1,0:T(8,128)S(1)}, u32[]{:S(2)}, u32[]{:S(2)}) %collective-permute-start.1) | collective-permute-done | bytes 622624 | tf_op jit(solution)/shard_map/ppermute | solution.py:22
  19.3 1.4 collective-permute-start.2
  20.7 1.5 collective-permute-start.3
  22.3 1.4 collective-permute-done.2
  26.5 0.2 add_select_fusion
  26.8 0.6 copy-done.3
  27.3 1.0 collective-permute-start.4
  28.4 4.2 %collective-permute-start.5 = (f32[19,1,32,256]{3,2,1,0:T(8,128)S(1)}, f32[19,1,32,256]{3,2,1,0:T(8,128)S(1)}, u32[]{:S(2)}, u32[]{:S(2)}) collective-permute-start(f32[19,1,32,256]{3,2,1,0:T(8,128)S(1)} %add_select_fusion), channel_id=1, source_target_pairs={{4,0},{8,4},{12,8},{16,12},{20,16},{24,20},{28,24},{32,28},{36,32}... | collective-permute-start | bytes 1867784 | tf_op jit(solution)/shard_map/ppermute | solution.py:22
  32.6 3.0 %collective-permute-done.4 = f32[19,1,32,256]{3,2,1,0:T(8,128)S(1)} collective-permute-done((f32[19,1,32,256]{3,2,1,0:T(8,128)S(1)}, f32[19,1,32,256]{3,2,1,0:T(8,128)S(1)}, u32[]{:S(2)}, u32[]{:S(2)}) %collective-permute-start.4) | collective-permute-done | bytes 622624 | tf_op jit(solution)/shard_map/ppermute | solution.py:20
  35.5 2.5 %collective-permute-done.5 = f32[19,1,32,256]{3,2,1,0:T(8,128)S(1)} collective-permute-done((f32[19,1,32,256]{3,2,1,0:T(8,128)S(1)}, f32[19,1,32,256]{3,2,1,0:T(8,128)S(1)}, u32[]{:S(2)}, u32[]{:S(2)}) %collective-permute-start.5) | collective-permute-done | bytes 622624 | tf_op jit(solution)/shard_map/ppermute | solution.py:22
  38.1 1.4 collective-permute-start.6
  39.5 1.4 collective-permute-start.7
  40.9 1.9 %collective-permute-done.6 = f32[19,3,1,256]{3,2,1,0:T(1,128)S(1)} collective-permute-done((f32[19,3,1,256]{3,2,1,0:T(1,128)S(1)}, f32[19,3,1,256]{3,2,1,0:T(1,128)S(1)}, u32[]{:S(2)}, u32[]{:S(2)}) %collective-permute-start.6) | collective-permute-done | bytes 58400 | tf_op jit(solution)/shard_map/ppermute | solution.py:20
  43.6 1.0 divide_reduce_fusion
  44.7 1.0 collective-permute-start.8
  45.7 7.6 %collective-permute-start.9 = (f32[19,1,32,256]{3,2,1,0:T(8,128)S(1)}, f32[19,1,32,256]{3,2,1,0:T(8,128)S(1)}, u32[]{:S(2)}, u32[]{:S(2)}) collective-permute-start(f32[19,1,32,256]{3,2,1,0:T(8,128)S(1)} %add_add_fusion.1), channel_id=1, source_target_pairs={{4,0},{8,4},{12,8},{16,12},{20,16},{24,20},{28,24},{32,28},{36,32}... | collective-permute-start | bytes 1867784 | tf_op jit(solution)/shard_map/ppermute | solution.py:22
  53.6 1.2 collective-permute-done.8
  54.8 0.6 collective-permute-done.9
  55.5 2.8 %collective-permute-start.10 = (f32[19,3,1,256]{3,2,1,0:T(1,128)S(1)}, f32[19,3,1,256]{3,2,1,0:T(1,128)S(1)}, u32[]{:S(2)}, u32[]{:S(2)}) collective-permute-start(f32[19,3,1,256]{3,2,1,0:T(1,128)S(1)} %get-tuple-element.104), channel_id=1, source_target_pairs={{1,0},{2,1},{3,2},{0,3},{5,4},{6,5},{7,6},{4,7},{9,8},{10,9},{11,1... | collective-permute-start | bytes 175112 | tf_op jit(solution)/shard_map/ppermute | solution.py:22
  58.4 1.2 collective-permute-done.10
  59.7 3.3 %collective-permute-done.11 = f32[19,3,1,256]{3,2,1,0:T(1,128)S(1)} collective-permute-done((f32[19,3,1,256]{3,2,1,0:T(1,128)S(1)}, f32[19,3,1,256]{3,2,1,0:T(1,128)S(1)}, u32[]{:S(2)}, u32[]{:S(2)}) %collective-permute-start.11) | collective-permute-done | bytes 58400 | tf_op jit(solution)/shard_map/ppermute | solution.py:20
  64.4 0.3 broadcast_multiply_fusion.4
  64.9 0.2 broadcast_multiply_fusion.5
  65.2 0.8 fusion.454
  66.0 0.6 copy-done.14
  66.7 0.3 add_add_fusion
  67.0 1.2 collective-permute-start.12
  68.2 11.0 %collective-permute-start.13 = (f32[19,1,32,256]{3,2,1,0:T(8,128)S(1)}, f32[19,1,32,256]{3,2,1,0:T(8,128)S(1)}, u32[]{:S(2)}, u32[]{:S(2)}) collective-permute-start(f32[19,1,32,256]{3,2,1,0:T(8,128)S(1)} %add_add_fusion), channel_id=1, source_target_pairs={{4,0},{8,4},{12,8},{16,12},{20,16},{24,20},{28,24},{32,28},{36,32}... | collective-permute-start | bytes 1867784 | tf_op jit(solution)/shard_map/ppermute | solution.py:22
  80.4 79.4 %psum.16 = f32[]{:T(128)} all-reduce(f32[]{:T(128)S(6)} %add.7467), channel_id=1, replica_groups=mesh['gz'=64,'gy'=4] {'gz','gy'}, use_global_device_ids=true, to_apply=%region_6.7 | all-reduce | flops 1 | bytes 8 | tf_op jit(solution)/shard_map/psum | solution.py:108
  161.0 1.5 collective-permute-start.15
  162.5 1.5 collective-permute-done.14
  164.1 1.2 collective-permute-done.15
  166.6 1.0 copy-done.8
  168.4 0.6 multiply_reduce_fusion.2
  169.0 0.3 broadcast_multiply_fusion.2
  169.3 0.3 broadcast_multiply_fusion.3
  169.6 0.3 broadcast_multiply_fusion.6
  169.9 0.7 copy-done.12
  170.6 0.6 fusion.467
  171.2 0.7 fusion.492
  171.8 1.1 add_divide_fusion
  (253 shorter events, 9.9 us)
Async XLA Ops:
  0.6 2.0 %copy-start = (f32[19,1,32,256]{3,2,1,0:T(8,128)S(1)}, f32[19,1,32,256]{3,2,1,0:T(8,128)}, u32[]{:S(2)}) copy-start(f32[19,1,32,256]{3,2,1,0:T(8,128)} %param.3) | copy-start | bytes 1867780
  4.0 0.8 copy-start.11
  4.1 0.8 copy-start.13
  5.1 0.8 copy-start.7
  5.1 1.0 copy-start.9
  6.1 13.1 %collective-permute-start = (f32[19,1,32,256]{3,2,1,0:T(8,128)S(1)}, f32[19,1,32,256]{3,2,1,0:T(8,128)S(1)}, u32[]{:S(2)}, u32[]{:S(2)}) collective-permute-start(f32[19,1,32,256]{3,2,1,0:T(8,128)S(1)} %add_select_fusion.1), channel_id=1, source_target_pairs={{0,4},{4,8},{8,12},{12,16},{16,20},{20,24},{24,28},{28,32},{32,36}... | collective-permute-start | bytes 1867784 | tf_op jit(solution)/shard_map/ppermute | solution.py:20
  9.1 10.0 %collective-permute-start.1 = (f32[19,1,32,256]{3,2,1,0:T(8,128)S(1)}, f32[19,1,32,256]{3,2,1,0:T(8,128)S(1)}, u32[]{:S(2)}, u32[]{:S(2)}) collective-permute-start(f32[19,1,32,256]{3,2,1,0:T(8,128)S(1)} %add_select_fusion.1), channel_id=1, source_target_pairs={{4,0},{8,4},{12,8},{16,12},{20,16},{24,20},{28,24},{32,28},{36,32}... | collective-permute-start | bytes 1867784 | tf_op jit(solution)/shard_map/ppermute | solution.py:22
  19.3 4.4 %collective-permute-start.2 = (f32[19,3,1,256]{3,2,1,0:T(1,128)S(1)}, f32[19,3,1,256]{3,2,1,0:T(1,128)S(1)}, u32[]{:S(2)}, u32[]{:S(2)}) collective-permute-start(f32[19,3,1,256]{3,2,1,0:T(1,128)S(1)} %get-tuple-element.111), channel_id=1, source_target_pairs={{0,1},{1,2},{2,3},{3,0},{4,5},{5,6},{6,7},{7,4},{8,9},{9,10},{10,1... | collective-permute-start | bytes 175112 | tf_op jit(solution)/shard_map/ppermute | solution.py:20
  20.7 3.0 %collective-permute-start.3 = (f32[19,3,1,256]{3,2,1,0:T(1,128)S(1)}, f32[19,3,1,256]{3,2,1,0:T(1,128)S(1)}, u32[]{:S(2)}, u32[]{:S(2)}) collective-permute-start(f32[19,3,1,256]{3,2,1,0:T(1,128)S(1)} %get-tuple-element.112), channel_id=1, source_target_pairs={{1,0},{2,1},{3,2},{0,3},{5,4},{6,5},{7,6},{4,7},{9,8},{10,9},{11,1... | collective-permute-start | bytes 175112 | tf_op jit(solution)/shard_map/ppermute | solution.py:22
  25.0 1.5 copy-start.5
  26.5 0.8 copy-start.3
  27.3 8.2 %collective-permute-start.4 = (f32[19,1,32,256]{3,2,1,0:T(8,128)S(1)}, f32[19,1,32,256]{3,2,1,0:T(8,128)S(1)}, u32[]{:S(2)}, u32[]{:S(2)}) collective-permute-start(f32[19,1,32,256]{3,2,1,0:T(8,128)S(1)} %add_select_fusion), channel_id=1, source_target_pairs={{0,4},{4,8},{8,12},{12,16},{16,20},{20,24},{24,28},{28,32},{32,36}... | collective-permute-start | bytes 1867784 | tf_op jit(solution)/shard_map/ppermute | solution.py:20
  28.4 9.7 %collective-permute-start.5 = (f32[19,1,32,256]{3,2,1,0:T(8,128)S(1)}, f32[19,1,32,256]{3,2,1,0:T(8,128)S(1)}, u32[]{:S(2)}, u32[]{:S(2)}) collective-permute-start(f32[19,1,32,256]{3,2,1,0:T(8,128)S(1)} %add_select_fusion), channel_id=1, source_target_pairs={{4,0},{8,4},{12,8},{16,12},{20,16},{24,20},{28,24},{32,28},{36,32}... | collective-permute-start | bytes 1867784 | tf_op jit(solution)/shard_map/ppermute | solution.py:22
  38.1 4.6 %collective-permute-start.6 = (f32[19,3,1,256]{3,2,1,0:T(1,128)S(1)}, f32[19,3,1,256]{3,2,1,0:T(1,128)S(1)}, u32[]{:S(2)}, u32[]{:S(2)}) collective-permute-start(f32[19,3,1,256]{3,2,1,0:T(1,128)S(1)} %get-tuple-element.107), channel_id=1, source_target_pairs={{0,1},{1,2},{2,3},{3,0},{4,5},{5,6},{6,7},{7,4},{8,9},{9,10},{10,1... | collective-permute-start | bytes 175112 | tf_op jit(solution)/shard_map/ppermute | solution.py:20
  39.5 3.5 %collective-permute-start.7 = (f32[19,3,1,256]{3,2,1,0:T(1,128)S(1)}, f32[19,3,1,256]{3,2,1,0:T(1,128)S(1)}, u32[]{:S(2)}, u32[]{:S(2)}) collective-permute-start(f32[19,3,1,256]{3,2,1,0:T(1,128)S(1)} %get-tuple-element.108), channel_id=1, source_target_pairs={{1,0},{2,1},{3,2},{0,3},{5,4},{6,5},{7,6},{4,7},{9,8},{10,9},{11,1... | collective-permute-start | bytes 175112 | tf_op jit(solution)/shard_map/ppermute | solution.py:22
  44.7 10.1 %collective-permute-start.8 = (f32[19,1,32,256]{3,2,1,0:T(8,128)S(1)}, f32[19,1,32,256]{3,2,1,0:T(8,128)S(1)}, u32[]{:S(2)}, u32[]{:S(2)}) collective-permute-start(f32[19,1,32,256]{3,2,1,0:T(8,128)S(1)} %add_add_fusion.1), channel_id=1, source_target_pairs={{0,4},{4,8},{8,12},{12,16},{16,20},{20,24},{24,28},{28,32},{32,36}... | collective-permute-start | bytes 1867784 | tf_op jit(solution)/shard_map/ppermute | solution.py:20
  45.7 9.7 %collective-permute-start.9 = (f32[19,1,32,256]{3,2,1,0:T(8,128)S(1)}, f32[19,1,32,256]{3,2,1,0:T(8,128)S(1)}, u32[]{:S(2)}, u32[]{:S(2)}) collective-permute-start(f32[19,1,32,256]{3,2,1,0:T(8,128)S(1)} %add_add_fusion.1), channel_id=1, source_target_pairs={{4,0},{8,4},{12,8},{16,12},{20,16},{24,20},{28,24},{32,28},{36,32}... | collective-permute-start | bytes 1867784 | tf_op jit(solution)/shard_map/ppermute | solution.py:22
  55.5 4.1 %collective-permute-start.10 = (f32[19,3,1,256]{3,2,1,0:T(1,128)S(1)}, f32[19,3,1,256]{3,2,1,0:T(1,128)S(1)}, u32[]{:S(2)}, u32[]{:S(2)}) collective-permute-start(f32[19,3,1,256]{3,2,1,0:T(1,128)S(1)} %get-tuple-element.104), channel_id=1, source_target_pairs={{1,0},{2,1},{3,2},{0,3},{5,4},{6,5},{7,6},{4,7},{9,8},{10,9},{11,1... | collective-permute-start | bytes 175112 | tf_op jit(solution)/shard_map/ppermute | solution.py:22
  58.4 4.6 %collective-permute-start.11 = (f32[19,3,1,256]{3,2,1,0:T(1,128)S(1)}, f32[19,3,1,256]{3,2,1,0:T(1,128)S(1)}, u32[]{:S(2)}, u32[]{:S(2)}) collective-permute-start(f32[19,3,1,256]{3,2,1,0:T(1,128)S(1)} %get-tuple-element.103), channel_id=1, source_target_pairs={{0,1},{1,2},{2,3},{3,0},{4,5},{5,6},{6,7},{7,4},{8,9},{9,10},{10,1... | collective-permute-start | bytes 175112 | tf_op jit(solution)/shard_map/ppermute | solution.py:20
  64.2 1.8 %copy-start.1 = (f32[19,1,32,256]{3,2,1,0:T(8,128)}, f32[19,1,32,256]{3,2,1,0:T(8,128)S(1)}, u32[]{:S(2)}) copy-start(f32[19,1,32,256]{3,2,1,0:T(8,128)S(1)} %constant_dynamic-update-slice_fusion.108) | copy-start | bytes 1867780
  66.0 0.7 copy-start.14
  67.0 93.8 %collective-permute-start.12 = (f32[19,1,32,256]{3,2,1,0:T(8,128)S(1)}, f32[19,1,32,256]{3,2,1,0:T(8,128)S(1)}, u32[]{:S(2)}, u32[]{:S(2)}) collective-permute-start(f32[19,1,32,256]{3,2,1,0:T(8,128)S(1)} %add_add_fusion), channel_id=1, source_target_pairs={{0,4},{4,8},{8,12},{12,16},{16,20},{20,24},{24,28},{28,32},{32,36}... | collective-permute-start | bytes 1867784 | tf_op jit(solution)/shard_map/ppermute | solution.py:20
  68.2 92.6 %collective-permute-start.13 = (f32[19,1,32,256]{3,2,1,0:T(8,128)S(1)}, f32[19,1,32,256]{3,2,1,0:T(8,128)S(1)}, u32[]{:S(2)}, u32[]{:S(2)}) collective-permute-start(f32[19,1,32,256]{3,2,1,0:T(8,128)S(1)} %add_add_fusion), channel_id=1, source_target_pairs={{4,0},{8,4},{12,8},{16,12},{20,16},{24,20},{28,24},{32,28},{36,32}... | collective-permute-start | bytes 1867784 | tf_op jit(solution)/shard_map/ppermute | solution.py:22
  160.9 3.1 %collective-permute-start.14 = (f32[19,3,1,256]{3,2,1,0:T(1,128)S(1)}, f32[19,3,1,256]{3,2,1,0:T(1,128)S(1)}, u32[]{:S(2)}, u32[]{:S(2)}) collective-permute-start(f32[19,3,1,256]{3,2,1,0:T(1,128)S(1)} %get-tuple-element.102), channel_id=1, source_target_pairs={{1,0},{2,1},{3,2},{0,3},{5,4},{6,5},{7,6},{4,7},{9,8},{10,9},{11,1... | collective-permute-start | bytes 175112 | tf_op jit(solution)/shard_map/ppermute | solution.py:22
  161.0 4.3 %collective-permute-start.15 = (f32[19,3,1,256]{3,2,1,0:T(1,128)S(1)}, f32[19,3,1,256]{3,2,1,0:T(1,128)S(1)}, u32[]{:S(2)}, u32[]{:S(2)}) collective-permute-start(f32[19,3,1,256]{3,2,1,0:T(1,128)S(1)} %get-tuple-element.101), channel_id=1, source_target_pairs={{0,1},{1,2},{2,3},{3,0},{4,5},{5,6},{6,7},{7,4},{8,9},{9,10},{10,1... | collective-permute-start | bytes 175112 | tf_op jit(solution)/shard_map/ppermute | solution.py:20
  166.5 1.1 copy-start.8
  166.6 1.3 copy-start.10
  166.6 1.4 copy-start.2
  166.6 1.6 copy-start.4
  166.6 1.8 %copy-start.6 = (f32[19,1,32,256]{3,2,1,0:T(8,128)S(1)}, f32[19,1,32,256]{3,2,1,0:T(8,128)}, u32[]{:S(2)}) copy-start(f32[19,1,32,256]{3,2,1,0:T(8,128)} %copy-done.5) | copy-start | bytes 1867780
  169.9 0.8 copy-start.12
where the time goes:
time: 174 us; the launch traced here: 173 us
  blocking collectives  79.4 us (46%)
  starting transfers between devices  39.4 us (23%)
  waiting for transfers between devices  27.2 us (16%)
  other arithmetic  13.8 us (8%)
  local copies, waits for them, and re-layouts  9.47 us (5%)
  between operations  3.7 us (2%)
    psum x1, blocking collectives, global_energy(): return lax.psum(value, ('gz', 'gy'))  79.4 us
    ppermute x8, starting transfers between devices, padded_2(): lax.ppermute(head, axis, [((i + 1) % count, i) for i in range(count)])  28.9 us
    ppermute x8, waiting for transfers between devices, padded_2(): lax.ppermute(head, axis, [((i + 1) % count, i) for i in range(count)])  15.3 us
    ppermute x8, waiting for transfers between devices, padded_2(): lax.ppermute(tail, axis, [(i, (i + 1) % count) for i in range(count)])  11.9 us
    ppermute x8, starting transfers between devices, padded_2(): lax.ppermute(tail, axis, [(i, (i + 1) % count) for i in range(count)])  10.5 us
    unnamed x76, local copies, waits for them, and re-layouts  6.28 us
    unnamed x79, other arithmetic  4.62 us
  transfers between devices with their start and end apart: 16, of which 11 were waited for; matrix products, arithmetic and copies ran while one was open for 1% of the time, Pallas kernels for 0%

commit v1 on v0

v1 whole, which is shorter than its diff:
```python
import functools

import jax
import jax.numpy as jnp
from jax import lax
from jax.experimental import pallas as pl
from jax.experimental.pallas import tpu as pltpu
from jax.sharding import PartitionSpec as P

STEPS = 2
OMEGA = 0.9
INLET_SPEED = 0.05
ROWS = 8
TOP = 8
MESH = pl.DeviceIdType.MESH


def velocity_table():
    velocities = [(0, 0, 0)]
    for axis in range(3):
        for sign in (1, -1):
            vector = [0, 0, 0]
            vector[axis] = sign
            velocities.append(tuple(vector))
    for first in range(3):
        for second in range(first + 1, 3):
            for sign_a in (1, -1):
                for sign_b in (1, -1):
                    vector = [0, 0, 0]
                    vector[first] = sign_a
                    vector[second] = sign_b
                    velocities.append(tuple(vector))
    weights = [1.0 / 3.0] + [1.0 / 18.0] * 6 + [1.0 / 36.0] * 12
    opposite = [velocities.index(tuple((-e for e in vector))) for vector in velocities]
    return (velocities, weights, opposite)


VEL, WEIGHT, OPP = velocity_table()
INDEX = {v: q for q, v in enumerate(VEL)}
PAIRS = [(q, OPP[q]) for q in range(19) if q < OPP[q]]
UP = [(0, 0, 1), (1, 0, 1), (-1, 0, 1), (0, 1, 1), (0, -1, 1)]
DOWN = [(0, 0, -1), (1, 0, -1), (-1, 0, -1), (0, 1, -1), (0, -1, -1)]
FLAT = [v for v in VEL if v[2] == 0]
FLAT_UP = [(0, 1, 0), (1, 1, 0), (-1, 1, 0)]
FLAT_DOWN = [(0, -1, 0), (1, -1, 0), (-1, -1, 0)]


def inlet_value(q):
    along = VEL[q][2] * INLET_SPEED
    return WEIGHT[q] * (1.0 + 3.0 * along + 4.5 * along * along - 1.5 * INLET_SPEED * INLET_SPEED)


def roll_x(value, shift):
    if shift == 0:
        return value
    return pltpu.roll(value, shift % value.shape[1], 1)


def signed(terms):
    total = None
    for sign, value in terms:
        if sign == 0:
            continue
        if total is None:
            total = value if sign > 0 else -value
        else:
            total = total + value if sign > 0 else total - value
    return total


def dot_c(c, vector):
    return signed([(c[i], vector[i]) for i in range(3)])


def collide(f, a, b, s, k):
    rho = functools.reduce(lambda p, q: p + q, f)
    m = [signed([(VEL[q][i], f[q]) for q in range(19)]) for i in range(3)]
    inv = 1.0 / rho
    u = [m[i] * inv for i in range(3)]
    speed = u[0] * u[0] + u[1] * u[1] + u[2] * u[2]
    brho = b * rho
    base = brho * (1.0 - 1.5 * speed)
    post = [None] * 19
    post[0] = (a + s) * f[0] + WEIGHT[0] * base + k * inlet_value(0)
    for q, o in PAIRS:
        w = WEIGHT[q]
        along = dot_c(VEL[q], u)
        even = w * base + (4.5 * w) * (brho * along) * along
        odd = (3.0 * w) * (brho * along)
        post[q] = a * f[q] + s * f[o] + (even + odd) + k * inlet_value(q)
        post[o] = a * f[o] + s * f[q] + (even - odd) + k * inlet_value(o)
    return rho, u, speed, post


def collide_adjoint(mu, f, rho, u, speed, a, b, s):
    plus = {q: mu[q] + mu[o] for q, o in PAIRS}
    minus = {q: mu[q] - mu[o] for q, o in PAIRS}

    def weighted(table, first, second=None):
        axial, diagonal = [], []
        for q, o in PAIRS:
            c = VEL[q]
            sign = c[first] if second is None else c[first] * c[second]
            (axial if WEIGHT[q] == WEIGHT[1] else diagonal).append((sign, table[q]))
        one, two = signed(axial), signed(diagonal)
        two = two * WEIGHT[7]
        return two if one is None else one * WEIGHT[1] + two

    axial = functools.reduce(lambda p, q: p + q, [plus[q] for q, o in PAIRS if WEIGHT[q] == WEIGHT[1]])
    diagonal = functools.reduce(lambda p, q: p + q, [plus[q] for q, o in PAIRS if WEIGHT[q] != WEIGHT[1]])
    big_a = WEIGHT[0] * mu[0] + WEIGHT[1] * axial + WEIGHT[7] * diagonal
    big_b = [3.0 * weighted(minus, i) for i in range(3)]
    big_c = {}
    for i in range(3):
        for j in range(i, 3):
            big_c[i, j] = big_c[j, i] = 4.5 * weighted(plus, i, j)
    cu = [sum(big_c[i, j] * u[j] for j in range(3)) for i in range(3)]
    quad = cu[0] * u[0] + cu[1] * u[1] + cu[2] * u[2] - 1.5 * speed * big_a
    by_rho = b * (big_a - quad)
    by_m = [b * (big_b[i] + 2.0 * cu[i] - 3.0 * big_a * u[i]) for i in range(3)]
    lam = [None] * 19
    lam[0] = (a + s) * mu[0] + by_rho
    same = mu[0] * f[0]
    cross = same
    for q, o in PAIRS:
        along = dot_c(VEL[q], by_m)
        lam[q] = a * mu[q] + s * mu[o] + (by_rho + along)
        lam[o] = a * mu[o] + s * mu[q] + (by_rho - along)
        same = same + (mu[q] * f[q] + mu[o] * f[o])
        cross = cross + (mu[q] * f[o] + mu[o] * f[q])
    total = rho * (big_a + big_b[0] * u[0] + big_b[1] * u[1] + big_b[2] * u[2] + quad)
    by_s = cross - ((1.0 - OMEGA) * same + OMEGA * total)
    return lam, by_s


def scratch_list(rows, cols, n_ar):
    f32 = jnp.float32
    padded = rows + 16
    names = {
        "f0": pltpu.VMEM((19, 1, rows, cols), f32),
        "sol": pltpu.VMEM((1, rows, cols), f32),
        "lab": pltpu.VMEM((1, rows, cols), jnp.int32),
        "coef": pltpu.VMEM((3, rows, cols), f32),
        "mom0": pltpu.VMEM((4, rows, cols), f32),
        "mom1": pltpu.VMEM((4, rows, cols), f32),
        "f1": pltpu.VMEM((19, rows, cols), f32),
        "ds": pltpu.VMEM((rows, cols), f32),
        "acc": pltpu.VMEM((ROWS, cols), f32),
        "lam": pltpu.VMEM((19, 1, rows, cols), f32),
        "sens": pltpu.VMEM((1, rows, cols), f32),
        "en": pltpu.VMEM((8, 128), f32),
        "in_sem": pltpu.SemaphoreType.DMA((3,)),
        "out_sem": pltpu.SemaphoreType.DMA((3,)),
        "ssem": pltpu.SemaphoreType.DMA((4, 14)),
        "rsem": pltpu.SemaphoreType.DMA((4, 14)),
        "part": pltpu.VMEM((6, padded, cols), f32),
        "grad": pltpu.VMEM((4, padded, cols), f32),
    }
    for r, fields, edge in ((0, 5, 3), (1, 4, 2), (2, 3, 2), (3, 5, 3)):
        names[f"up{r}"] = pltpu.VMEM((fields, rows, cols), f32)
        names[f"dn{r}"] = pltpu.VMEM((fields, rows, cols), f32)
        names[f"rup{r}"] = pltpu.VMEM((fields, padded, cols), f32)
        names[f"rdn{r}"] = pltpu.VMEM((fields, padded, cols), f32)
        for name in ("yu", "yd", "ryu", "ryd"):
            names[f"{name}{r}"] = pltpu.VMEM((edge, cols), f32)
        for i in range(4):
            names[f"dg{r}{i}"] = pltpu.VMEM((1, cols), f32)
            names[f"rdg{r}{i}"] = pltpu.VMEM((1, cols), f32)
    for r in (0, 3):
        names[f"flat{r}"] = pltpu.VMEM((9, padded, cols), f32)
    for stage, count in enumerate(n_ar):
        names[f"ar{stage}"] = pltpu.VMEM((1, 128), f32)
        names[f"ras{stage}"] = pltpu.SemaphoreType.DMA((count,))
        names[f"rar{stage}"] = pltpu.SemaphoreType.DMA((count,))
        for i in range(count):
            names[f"arr{stage}_{i}"] = pltpu.VMEM((1, 128), f32)
    return names


def kernel(names, sizes, pop_ref, sol_ref, lab_ref, lam_ref, sens_ref, en_ref, *refs):
    S = dict(zip(names, refs))
    n_gz, n_gy, n_x, n_z, n_core = sizes
    rows, cols = S["ds"].shape
    chunks = rows // ROWS
    last = TOP + rows
    gz = lax.axis_index("gz")
    gy = lax.axis_index("gy")

    loads = [
        pltpu.make_async_copy(pop_ref, S["f0"], S["in_sem"].at[0]),
        pltpu.make_async_copy(sol_ref, S["sol"], S["in_sem"].at[1]),
        pltpu.make_async_copy(lab_ref, S["lab"], S["in_sem"].at[2]),
    ]
    for load in loads:
        load.start()

    def at(dz, dy):
        return (lax.rem(gz + dz + n_gz, n_gz), lax.rem(gy + dy + n_gy, n_gy))

    core = lax.rem(gz, n_core)
    zpos = lax.rem(gz // n_core, n_z)
    xpos = gz // (n_core * n_z)

    def place(dx, dz, dcore, dy):
        x = lax.rem(xpos + dx, n_x)
        z = lax.rem(zpos + dz, n_z)
        c = lax.rem(core + dcore, n_core)
        return ((x * n_z + z) * n_core + c, lax.rem(gy + dy, n_gy))

    stages = [
        [place(0, 0, dc, dy) for dc in range(n_core) for dy in range(n_gy) if (dc, dy) != (0, 0)],
        [place(0, dz, 0, 0) for dz in range(1, n_z)],
        [place(dx, 0, 0, 0) for dx in range(1, n_x)],
    ]
    near = [at(dz, dy) for dz, dy in ((1, 0), (-1, 0), (0, 1), (0, -1), (1, 1), (1, -1), (-1, 1), (-1, -1))]
    barrier = pltpu.get_barrier_semaphore()
    greeted = near + [d for stage in stages for d in stage]
    for device in greeted:
        pl.semaphore_signal(barrier, inc=1, device_id=device, device_id_type=MESH)

    def send(src, dst, r, i, device):
        copy = pltpu.make_async_remote_copy(
            src_ref=src,
            dst_ref=dst,
            send_sem=S["ssem"].at[r, i],
            recv_sem=S["rsem"].at[r, i],
            device_id=device,
            device_id_type=MESH,
        )
        copy.start()
        started[r].append(copy)

    started = [[], [], [], []]

    def send_bulk(r, k):
        src, dst = pl.ds(k * ROWS, ROWS), pl.ds(TOP + k * ROWS, ROWS)
        send(S[f"up{r}"].at[:, src, :], S[f"rup{r}"].at[:, dst, :], r, k, at(1, 0))
        send(S[f"dn{r}"].at[:, src, :], S[f"rdn{r}"].at[:, dst, :], r, chunks + k, at(-1, 0))

    def send_edges(r):
        base = 2 * chunks
        send(S[f"yu{r}"], S[f"ryu{r}"], r, base, at(0, 1))
        send(S[f"yd{r}"], S[f"ryd{r}"], r, base + 1, at(0, -1))
        for i, (dz, dy) in enumerate(((1, 1), (1, -1), (-1, 1), (-1, -1))):
            send(S[f"dg{r}{i}"], S[f"rdg{r}{i}"], r, base + 2 + i, at(dz, dy))

    def receive(r):
        for copy in started[r]:
            copy.wait_recv()

    def interior(k):
        return pl.ds(TOP + k * ROWS, ROWS)

    def moved(k, dy):
        return pl.ds(TOP + k * ROWS - dy, ROWS)

    def emit_populations(r, k, values, sense):
        here = pl.ds(k * ROWS, ROWS)
        for name, table in (("up", UP), ("dn", DOWN)):
            for i, d in enumerate(table):
                q = INDEX[tuple(sense * e for e in d)]
                value = roll_x(values[q], d[0])
                S[f"{name}{r}"][i, here, :] = value
                slot = {("up", 1): 0, ("up", -1): 1, ("dn", 1): 2, ("dn", -1): 3}.get((name, d[1]))
                if d[1] == 1 and k == chunks - 1:
                    S[f"dg{r}{slot}"][...] = value[ROWS - 1 :, :]
                if d[1] == -1 and k == 0:
                    S[f"dg{r}{slot}"][...] = value[:1, :]
        for i, d in enumerate(FLAT):
            q = INDEX[tuple(sense * e for e in d)]
            value = roll_x(values[q], d[0])
            S[f"flat{r}"][i, interior(k), :] = value
            if d[1] == 1 and k == chunks - 1:
                j = FLAT_UP.index(d)
                S[f"yu{r}"][j : j + 1, :] = value[ROWS - 1 :, :]
            if d[1] == -1 and k == 0:
                j = FLAT_DOWN.index(d)
                S[f"yd{r}"][j : j + 1, :] = value[:1, :]

    def place_edges(r):
        for i, name, row in ((0, "rup", TOP - 1), (1, "rup", last), (2, "rdn", TOP - 1), (3, "rdn", last)):
            slot = 3 if i % 2 == 0 else 4
            S[f"{name}{r}"][slot, pl.ds(row, 1), :] = S[f"rdg{r}{i}"][...]
        for j in range(3):
            S[f"flat{r}"][FLAT.index(FLAT_UP[j]), pl.ds(TOP - 1, 1), :] = S[f"ryu{r}"][j : j + 1, :]
            S[f"flat{r}"][FLAT.index(FLAT_DOWN[j]), pl.ds(last, 1), :] = S[f"ryd{r}"][j : j + 1, :]

    def gather_populations(r, k, sense):
        values = [None] * 19
        for name, table in (("rup", UP), ("rdn", DOWN), ("flat", FLAT)):
            for i, d in enumerate(table):
                q = INDEX[tuple(sense * e for e in d)]
                values[q] = S[f"{name}{r}"][i, moved(k, d[1]), :]
        return values

    def coefficients(k):
        here = pl.ds(k * ROWS, ROWS)
        return [S["coef"][i, here, :] for i in range(3)]

    def inlet(k):
        return jnp.where(S["lab"][0, pl.ds(k * ROWS, ROWS), :] == 3, 1.0, 0.0)

    for load in loads:
        load.wait()
    pl.semaphore_wait(barrier, len(greeted))
    for k in range(chunks):
        here = pl.ds(k * ROWS, ROWS)
        label = S["lab"][0, here, :]
        s = jnp.where(label == 1, S["sol"][0, here, :], jnp.where(label == 2, 1.0, 0.0))
        free = jnp.where(label == 3, 0.0, 1.0 - s)
        b = jnp.where(label == 4, free, OMEGA * free)
        a = jnp.where(label == 4, 0.0, (1.0 - OMEGA) * free)
        for i, value in enumerate((a, b, s)):
            S["coef"][i, here, :] = value
        f = [S["f0"][q, 0, here, :] for q in range(19)]
        rho, u, speed, post = collide(f, a, b, s, inlet(k))
        for i, value in enumerate((rho, *u)):
            S["mom0"][i, here, :] = value
        emit_populations(0, k, post, 1)
        send_bulk(0, k)
    send_edges(0)

    receive(0)
    place_edges(0)
    for k in range(chunks):
        here = pl.ds(k * ROWS, ROWS)
        a, b, s = coefficients(k)
        f = gather_populations(0, k, 1)
        for q in range(19):
            S["f1"][q, here, :] = f[q]
        rho, u, speed, post = collide(f, a, b, s, inlet(k))
        for i, value in enumerate((rho, *u)):
            S["mom1"][i, here, :] = value
        flow = rho * speed
        S["ds"][here, :] = -flow
        energy = (1.0 - s) * flow
        S["acc"][...] = energy if k == 0 else S["acc"][...] + energy

        def three(cy, cz):
            mid = post[INDEX[0, cy, cz]]
            right = roll_x(post[INDEX[1, cy, cz]], 1)
            left = roll_x(post[INDEX[-1, cy, cz]], -1)
            return mid + right + left, right - left

        for name, cz, slot in (("up", 1, 0), ("dn", -1, 2)):
            total, along = three(0, cz)
            ahead, behind = post[INDEX[0, 1, cz]], post[INDEX[0, -1, cz]]
            for i, value in enumerate((total, along, ahead, behind)):
                S[f"{name}1"][i, here, :] = value
            if k == chunks - 1:
                S[f"dg1{slot}"][...] = ahead[ROWS - 1 :, :]
            if k == 0:
                S[f"dg1{slot + 1}"][...] = behind[:1, :]
        send_bulk(1, k)
        for j, cy in enumerate((0, 1, -1)):
            total, along = three(cy, 0)
            S["part"][2 * j, interior(k), :] = total
            S["part"][2 * j + 1, interior(k), :] = along
            if cy == 1 and k == chunks - 1:
                S["yu1"][0:1, :] = total[ROWS - 1 :, :]
                S["yu1"][1:2, :] = along[ROWS - 1 :, :]
            if cy == -1 and k == 0:
                S["yd1"][0:1, :] = total[:1, :]
                S["yd1"][1:2, :] = along[:1, :]
    send_edges(1)

    receive(1)
    for i, name, row in ((0, "rup1", TOP - 1), (1, "rup1", last), (2, "rdn1", TOP - 1), (3, "rdn1", last)):
        S[name][2 + i % 2, pl.ds(row, 1), :] = S[f"rdg1{i}"][...]
    for j in range(2):
        S["part"][2 + j, pl.ds(TOP - 1, 1), :] = S["ryu1"][j : j + 1, :]
        S["part"][4 + j, pl.ds(last, 1), :] = S["ryd1"][j : j + 1, :]
    for k in range(chunks):
        here = pl.ds(k * ROWS, ROWS)
        s = S["coef"][2, here, :]
        above, below = {}, {}
        for table, name in ((above, "rup1"), (below, "rdn1")):
            table["sum"] = S[name][0, interior(k), :]
            table["x"] = S[name][1, interior(k), :]
            table["ahead"] = S[name][2, moved(k, 1), :]
            table["behind"] = S[name][3, moved(k, -1), :]
            table["all"] = table["sum"] + (table["ahead"] + table["behind"])
        mid, mid_x = S["part"][0, interior(k), :], S["part"][1, interior(k), :]
        ahead, ahead_x = S["part"][2, moved(k, 1), :], S["part"][3, moved(k, 1), :]
        behind, behind_x = S["part"][4, moved(k, -1), :], S["part"][5, moved(k, -1), :]
        rho = above["all"] + below["all"] + (mid + (ahead + behind))
        inv = 1.0 / rho
        ux = (above["x"] + below["x"] + (mid_x + (ahead_x + behind_x))) * inv
        uy = ((above["ahead"] - above["behind"]) + (below["ahead"] - below["behind"]) + (ahead - behind)) * inv
        uz = (above["all"] - below["all"]) * inv
        speed = ux * ux + uy * uy + uz * uz
        flow = rho * speed
        S["ds"][here, :] = S["ds"][here, :] - flow
        S["acc"][...] = S["acc"][...] + (1.0 - s) * flow
        e = (1.0 - s) * speed
        twice = 2.0 * (1.0 - s)
        x, y, z = twice * ux, twice * uy, twice * uz
        for name, w, slot in (("up", -z - e, 0), ("dn", z - e, 2)):
            for i, value in enumerate((x, y, w)):
                S[f"{name}2"][i, here, :] = value
            if k == chunks - 1:
                S[f"dg2{slot}"][...] = (w - y)[ROWS - 1 :, :]
            if k == 0:
                S[f"dg2{slot + 1}"][...] = (w + y)[:1, :]
        send_bulk(2, k)
        for i, value in enumerate((x, y - e, -y - e, e)):
            S["grad"][i, interior(k), :] = value
        if k == chunks - 1:
            S["yu2"][0:1, :] = x[ROWS - 1 :, :]
            S["yu2"][1:2, :] = (-y - e)[ROWS - 1 :, :]
        if k == 0:
            S["yd2"][0:1, :] = x[:1, :]
            S["yd2"][1:2, :] = (y - e)[:1, :]
    send_edges(2)

    sums = []

    def reduce_send(stage, value):
        S[f"ar{stage}"][...] = value
        for i, device in enumerate(stages[stage]):
            copy = pltpu.make_async_remote_copy(
                src_ref=S[f"ar{stage}"],
                dst_ref=S[f"arr{stage}_{i}"],
                send_sem=S[f"ras{stage}"].at[i],
                recv_sem=S[f"rar{stage}"].at[i],
                device_id=device,
                device_id_type=MESH,
            )
            copy.start()
            sums.append((stage, copy))

    def reduce_receive(stage):
        value = S[f"ar{stage}"][...]
        for which, copy in sums:
            if which == stage:
                copy.wait_recv()
        for i in range(len(stages[stage])):
            value = value + S[f"arr{stage}_{i}"][...]
        return value

    acc = S["acc"][...]
    acc = functools.reduce(lambda p, q: p + q, [acc[:, i : i + 128] for i in range(0, cols, 128)])
    reduce_send(0, jnp.sum(acc, axis=0, keepdims=True))

    zero_row = jnp.zeros((1, cols), jnp.float32)
    reduce_send(1, reduce_receive(0))
    receive(2)
    for i, name, row in ((0, "rup2", TOP - 1), (1, "rup2", last), (2, "rdn2", TOP - 1), (3, "rdn2", last)):
        S[name][2, pl.ds(row, 1), :] = S[f"rdg2{i}"][...]
        S[name][1, pl.ds(row, 1), :] = zero_row
    for j, slot in ((0, 0), (1, 2)):
        S["grad"][slot, pl.ds(TOP - 1, 1), :] = S["ryu2"][j : j + 1, :]
    for j, slot in ((0, 0), (1, 1)):
        S["grad"][slot, pl.ds(last, 1), :] = S["ryd2"][j : j + 1, :]
    for k in range(chunks):
        here = pl.ds(k * ROWS, ROWS)
        a, b, s = coefficients(k)
        mu = [None] * 19
        for name, cz in (("rup2", -1), ("rdn2", 1)):
            x, w = S[name][0, interior(k), :], S[name][2, interior(k), :]
            mu[INDEX[0, 0, cz]] = w
            mu[INDEX[1, 0, cz]] = roll_x(w + x, -1)
            mu[INDEX[-1, 0, cz]] = roll_x(w - x, 1)
            mu[INDEX[0, 1, cz]] = S[name][2, moved(k, -1), :] + S[name][1, moved(k, -1), :]
            mu[INDEX[0, -1, cz]] = S[name][2, moved(k, 1), :] - S[name][1, moved(k, 1), :]
        for cy, slot in ((0, 3), (1, 1), (-1, 2)):
            x, w = S["grad"][0, moved(k, -cy), :], S["grad"][slot, moved(k, -cy), :]
            w = -w if cy == 0 else w
            mu[INDEX[0, cy, 0]] = w
            mu[INDEX[1, cy, 0]] = roll_x(w + x, -1)
            mu[INDEX[-1, cy, 0]] = roll_x(w - x, 1)
        f = [S["f1"][q, here, :] for q in range(19)]
        rho, u = S["mom1"][0, here, :], [S["mom1"][i, here, :] for i in (1, 2, 3)]
        speed = u[0] * u[0] + u[1] * u[1] + u[2] * u[2]
        lam, by_s = collide_adjoint(mu, f, rho, u, speed, a, b, s)
        S["ds"][here, :] = S["ds"][here, :] + by_s
        twice = 2.0 * (1.0 - s)
        twice_u = [twice * u[i] for i in range(3)]
        e = (1.0 - s) * speed
        lam[0] = lam[0] - e
        for q, o in PAIRS:
            along = dot_c(VEL[q], twice_u)
            lam[q] = lam[q] + (along - e)
            lam[o] = lam[o] - (along + e)
        emit_populations(3, k, lam, -1)
        send_bulk(3, k)
    send_edges(3)

    reduce_send(2, reduce_receive(1))
    receive(3)
    place_edges(3)
    for k in range(chunks):
        here = pl.ds(k * ROWS, ROWS)
        a, b, s = coefficients(k)
        mu = gather_populations(3, k, -1)
        f = [S["f0"][q, 0, here, :] for q in range(19)]
        rho, u = S["mom0"][0, here, :], [S["mom0"][i, here, :] for i in (1, 2, 3)]
        speed = u[0] * u[0] + u[1] * u[1] + u[2] * u[2]
        lam, by_s = collide_adjoint(mu, f, rho, u, speed, a, b, s)
        for q in range(19):
            S["lam"][q, 0, here, :] = lam[q]
        S["sens"][0, here, :] = jnp.where(S["lab"][0, here, :] == 1, S["ds"][here, :] + by_s, 0.0)
    stores = [
        pltpu.make_async_copy(S["lam"], lam_ref, S["out_sem"].at[0]),
        pltpu.make_async_copy(S["sens"], sens_ref, S["out_sem"].at[1]),
        pltpu.make_async_copy(S["en"], en_ref, S["out_sem"].at[2]),
    ]
    stores[0].start()
    stores[1].start()
    total = jnp.sum(reduce_receive(2), axis=1, keepdims=True)
    S["en"][...] = jnp.broadcast_to(total, (8, 128))
    stores[2].start()
    for copies in started:
        for copy in copies:
            copy.wait_send()
    for stage, copy in sums:
        copy.wait_send()
    for store in stores:
        store.wait()


def on_device(sizes, populations, solid_fraction, labels):
    rows, cols = solid_fraction.shape[1:]
    n_gz, n_gy, n_x, n_z, n_core = sizes
    names = scratch_list(rows, cols, (n_core * n_gy - 1, n_z - 1, n_x - 1))
    f32 = jnp.float32
    anywhere = pl.BlockSpec(memory_space=pl.ANY)
    lam, sens, total = pl.pallas_call(
        functools.partial(kernel, tuple(names), sizes),
        out_shape=(
            jax.ShapeDtypeStruct(populations.shape, f32),
            jax.ShapeDtypeStruct(solid_fraction.shape, f32),
            jax.ShapeDtypeStruct((8, 128), f32),
        ),
        in_specs=[anywhere] * 3,
        out_specs=(anywhere,) * 3,
        scratch_shapes=list(names.values()),
        compiler_params=pltpu.CompilerParams(
            collective_id=0, has_side_effects=True, vmem_limit_bytes=24 * 1024 * 1024
        ),
        name="lattice",
    )(populations, solid_fraction, labels)
    cells = n_gz * n_gy * rows * cols
    mean_energy = total[0, 0] / (STEPS * cells)
    return (sens / mean_energy, lam / mean_energy)


def solution(mesh):
    n_gz, n_gy = mesh.shape["gz"], mesh.shape["gy"]
    n_core = 2
    n_z = 8 if n_gz % 16 == 0 else n_gz // 2
    n_x = n_gz // (n_core * n_z)
    in_specs = (P(None, "gz", "gy", None), P("gz", "gy", None), P("gz", "gy", None))
    out_specs = (P("gz", "gy", None), P(None, "gz", "gy", None))
    return jax.shard_map(
        functools.partial(on_device, (n_gz, n_gy, n_x, n_z, n_core)),
        mesh=mesh,
        in_specs=in_specs,
        out_specs=out_specs,
        check_vma=False,
    )
```

time: 174 us -> 43.1 us (0.25)
  the two profiles are of different devices: /device:TPU:1 before, /device:TPU:0 now
where the time goes in v1:
time: 43.1 us; the launch traced here: 42.8 us
  Pallas kernels  36.9 us (86%)
  local copies, waits for them, and re-layouts  3.1 us (7%)
  other arithmetic  1.52 us (4%)
  between operations  1.3 us (3%)
    pallas_call x1, Pallas kernels, on_device(): pl.pallas_call(functools.partial(kernel, tuple(names), sizes), out_shape=...  36.9 us
    unnamed x6, local copies, waits for them, and re-layouts  2.58 us
    div x2, other arithmetic, on_device(): return (sens / mean_energy, lam / mean_energy)  1.52 us

profile of v1, /device:TPU:0, one launch (start us, length us, event | category | flops | bytes accessed | tf_op | source)
XLA Modules:
  0.0 42.8 jit_solution(530489794911457593)
XLA Ops:
  0.6 0.0 copy-start
  0.6 1.1 %copy-done = f32[19,1,32,256]{3,2,1,0:T(8,128)S(1)} copy-done((f32[19,1,32,256]{3,2,1,0:T(8,128)S(1)}, f32[19,1,32,256]{3,2,1,0:T(8,128)}, u32[]{:S(2)}) %copy-start) | copy-done | bytes 622616
  1.7 0.0 copy-start.1
  1.7 0.8 %copy-done.1 = f32[1,32,256]{2,1,0:T(8,128)S(1)} copy-done((f32[1,32,256]{2,1,0:T(8,128)S(1)}, f32[1,32,256]{2,1,0:T(8,128)}, u32[]{:S(2)}) %copy-start.1) | copy-done | bytes 32792
  2.5 0.0 copy-start.2
  2.5 0.8 %copy-done.2 = s32[1,32,256]{2,1,0:T(8,128)S(1)} copy-done((s32[1,32,256]{2,1,0:T(8,128)S(1)}, s32[1,32,256]{2,1,0:T(8,128)}, u32[]{:S(2)}) %copy-start.2) | copy-done | bytes 32792
  3.2 36.9 %lattice.1 = (f32[19,1,32,256]{3,2,1,0:T(8,128)S(1)}, f32[1,32,256]{2,1,0:T(8,128)S(1)}, f32[8,128]{1,0:T(8,128)S(1)}) custom-call(f32[19,1,32,256]{3,2,1,0:T(8,128)S(1)} %copy-done, f32[1,32,256]{2,1,0:T(8,128)S(1)} %copy-done.1, s32[1,32,256]{2,1,0:T(8,128)S(1)} %copy-done.2), custom_call_target="tpu_custom_call" | custom-call | tf_op jit(solution)/shard_map/lattice/pallas_call | solution.py:528
  40.2 0.5 %slice.3 = f32[1,1]{1,0:T(1,128)} slice(f32[8,128]{1,0:T(8,128)S(1)} %get-tuple-element.6), slice={[0:1], [0:1]} | slice | bytes 8 | tf_op jit(solution)/shard_map/slice | solution.py:544
  41.3 0.6 %broadcast_divide_fusion.1 = f32[1,32,256]{2,1,0:T(8,128)} fusion(f32[1,32,256]{2,1,0:T(8,128)S(1)} %get-tuple-element.5, f32[]{:T(128)} %bitcast), kind=kLoop, calls=%fused_computation.1 | loop fusion | flops 8192 | bytes 65540 | tf_op jit(solution)/shard_map/div | solution.py:545
  41.9 0.9 %broadcast_divide_fusion = f32[19,1,32,256]{3,2,1,0:T(8,128)} fusion(f32[19,1,32,256]{3,2,1,0:T(8,128)S(1)} %get-tuple-element.7, f32[]{:T(128)} %bitcast), kind=kLoop, calls=%fused_computation | loop fusion | flops 155648 | bytes 1245188 | tf_op jit(solution)/shard_map/div | solution.py:545
Async XLA Ops:
  0.6 1.1 %copy-start = (f32[19,1,32,256]{3,2,1,0:T(8,128)S(1)}, f32[19,1,32,256]{3,2,1,0:T(8,128)}, u32[]{:S(2)}) copy-start(f32[19,1,32,256]{3,2,1,0:T(8,128)} %pop_ref.1) | copy-start | bytes 1867780
  1.7 0.8 %copy-start.1 = (f32[1,32,256]{2,1,0:T(8,128)S(1)}, f32[1,32,256]{2,1,0:T(8,128)}, u32[]{:S(2)}) copy-start(f32[1,32,256]{2,1,0:T(8,128)} %sol_ref.1) | copy-start | bytes 98308
  2.5 0.8 %copy-start.2 = (s32[1,32,256]{2,1,0:T(8,128)S(1)}, s32[1,32,256]{2,1,0:T(8,128)}, u32[]{:S(2)}) copy-start(s32[1,32,256]{2,1,0:T(8,128)} %lab_ref.1) | copy-start | bytes 98308

commit v2 on v1

--- a/solution.py
+++ b/solution.py
@@ -146,11 +146,7 @@
         "f1": pltpu.VMEM((19, rows, cols), f32),
         "ds": pltpu.VMEM((rows, cols), f32),
         "acc": pltpu.VMEM((ROWS, cols), f32),
-        "lam": pltpu.VMEM((19, 1, rows, cols), f32),
-        "sens": pltpu.VMEM((1, rows, cols), f32),
-        "en": pltpu.VMEM((8, 128), f32),
         "in_sem": pltpu.SemaphoreType.DMA((3,)),
-        "out_sem": pltpu.SemaphoreType.DMA((3,)),
         "ssem": pltpu.SemaphoreType.DMA((4, 14)),
         "rsem": pltpu.SemaphoreType.DMA((4, 14)),
         "part": pltpu.VMEM((6, padded, cols), f32),
@@ -182,6 +178,7 @@
     n_gz, n_gy, n_x, n_z, n_core = sizes
     rows, cols = S["ds"].shape
     chunks = rows // ROWS
+    order = [0, chunks - 1, *range(1, chunks - 1)]
     last = TOP + rows
     gz = lax.axis_index("gz")
     gy = lax.axis_index("gy")
@@ -243,6 +240,11 @@
         send(S[f"yd{r}"], S[f"ryd{r}"], r, base + 1, at(0, -1))
         for i, (dz, dy) in enumerate(((1, 1), (1, -1), (-1, 1), (-1, -1))):
             send(S[f"dg{r}{i}"], S[f"rdg{r}{i}"], r, base + 2 + i, at(dz, dy))
+
+    def send_chunk(r, k):
+        if k == chunks - 1:
+            send_edges(r)
+        send_bulk(r, k)
 
     def receive(r):
         for copy in started[r]:
@@ -303,7 +305,7 @@
     for load in loads:
         load.wait()
     pl.semaphore_wait(barrier, len(greeted))
-    for k in range(chunks):
+    for k in order:
         here = pl.ds(k * ROWS, ROWS)
         label = S["lab"][0, here, :]
         s = jnp.where(label == 1, S["sol"][0, here, :], jnp.where(label == 2, 1.0, 0.0))
@@ -317,12 +319,11 @@
         for i, value in enumerate((rho, *u)):
             S["mom0"][i, here, :] = value
         emit_populations(0, k, post, 1)
-        send_bulk(0, k)
-    send_edges(0)
+        send_chunk(0, k)
 
     receive(0)
     place_edges(0)
-    for k in range(chunks):
+    for k in order:
         here = pl.ds(k * ROWS, ROWS)
         a, b, s = coefficients(k)
         f = gather_populations(0, k, 1)
@@ -351,7 +352,6 @@
                 S[f"dg1{slot}"][...] = ahead[ROWS - 1 :, :]
             if k == 0:
                 S[f"dg1{slot + 1}"][...] = behind[:1, :]
-        send_bulk(1, k)
         for j, cy in enumerate((0, 1, -1)):
             total, along = three(cy, 0)
             S["part"][2 * j, interior(k), :] = total
@@ -362,7 +362,7 @@
             if cy == -1 and k == 0:
                 S["yd1"][0:1, :] = total[:1, :]
                 S["yd1"][1:2, :] = along[:1, :]
-    send_edges(1)
+        send_chunk(1, k)
 
     receive(1)
     for i, name, row in ((0, "rup1", TOP - 1), (1, "rup1", last), (2, "rdn1", TOP - 1), (3, "rdn1", last)):
@@ -370,7 +370,7 @@
     for j in range(2):
         S["part"][2 + j, pl.ds(TOP - 1, 1), :] = S["ryu1"][j : j + 1, :]
         S["part"][4 + j, pl.ds(last, 1), :] = S["ryd1"][j : j + 1, :]
-    for k in range(chunks):
+    for k in order:
         here = pl.ds(k * ROWS, ROWS)
         s = S["coef"][2, here, :]
         above, below = {}, {}
@@ -402,7 +402,6 @@
                 S[f"dg2{slot}"][...] = (w - y)[ROWS - 1 :, :]
             if k == 0:
                 S[f"dg2{slot + 1}"][...] = (w + y)[:1, :]
-        send_bulk(2, k)
         for i, value in enumerate((x, y - e, -y - e, e)):
             S["grad"][i, interior(k), :] = value
         if k == chunks - 1:
@@ -411,7 +410,7 @@
         if k == 0:
             S["yd2"][0:1, :] = x[:1, :]
             S["yd2"][1:2, :] = (y - e)[:1, :]
-    send_edges(2)
+        send_chunk(2, k)
 
     sums = []
 
@@ -452,7 +451,7 @@
         S["grad"][slot, pl.ds(TOP - 1, 1), :] = S["ryu2"][j : j + 1, :]
     for j, slot in ((0, 0), (1, 1)):
         S["grad"][slot, pl.ds(last, 1), :] = S["ryd2"][j : j + 1, :]
-    for k in range(chunks):
+    for k in order:
         here = pl.ds(k * ROWS, ROWS)
         a, b, s = coefficients(k)
         mu = [None] * 19
@@ -483,13 +482,12 @@
             lam[q] = lam[q] + (along - e)
             lam[o] = lam[o] - (along + e)
         emit_populations(3, k, lam, -1)
-        send_bulk(3, k)
-    send_edges(3)
+        send_chunk(3, k)
 
     reduce_send(2, reduce_receive(1))
     receive(3)
     place_edges(3)
-    for k in range(chunks):
+    for k in order:
         here = pl.ds(k * ROWS, ROWS)
         a, b, s = coefficients(k)
         mu = gather_populations(3, k, -1)
@@ -498,23 +496,32 @@
         speed = u[0] * u[0] + u[1] * u[1] + u[2] * u[2]
         lam, by_s = collide_adjoint(mu, f, rho, u, speed, a, b, s)
         for q in range(19):
-            S["lam"][q, 0, here, :] = lam[q]
-        S["sens"][0, here, :] = jnp.where(S["lab"][0, here, :] == 1, S["ds"][here, :] + by_s, 0.0)
-    stores = [
-        pltpu.make_async_copy(S["lam"], lam_ref, S["out_sem"].at[0]),
-        pltpu.make_async_copy(S["sens"], sens_ref, S["out_sem"].at[1]),
-        pltpu.make_async_copy(S["en"], en_ref, S["out_sem"].at[2]),
-    ]
-    stores[0].start()
-    stores[1].start()
+            lam_ref[q, 0, here, :] = lam[q]
+        sens_ref[0, here, :] = jnp.where(S["lab"][0, here, :] == 1, S["ds"][here, :] + by_s, 0.0)
     total = jnp.sum(reduce_receive(2), axis=1, keepdims=True)
-    S["en"][...] = jnp.broadcast_to(total, (8, 128))
-    stores[2].start()
+    en_ref[...] = jnp.broadcast_to(total, en_ref.shape)
     for copies in started:
         for copy in copies:
             copy.wait_send()
     for stage, copy in sums:
         copy.wait_send()
+
+
+def finish(scale, lam_ref, sens_ref, en_ref, out_sens, out_lam, lam, sens, sems):
+    inv = 1.0 / (en_ref[...] * scale)
+    rows = sens.shape[1]
+    stores = [
+        pltpu.make_async_copy(lam.at[pl.ds(q, 1)], out_lam.at[pl.ds(q, 1)], sems.at[q]) for q in range(19)
+    ] + [pltpu.make_async_copy(sens, out_sens, sems.at[19])]
+    for q in range(19):
+        for k in range(rows // ROWS):
+            here = pl.ds(k * ROWS, ROWS)
+            lam[q, 0, here, :] = lam_ref[q, 0, here, :] * inv
+        stores[q].start()
+    for k in range(rows // ROWS):
+        here = pl.ds(k * ROWS, ROWS)
+        sens[0, here, :] = sens_ref[0, here, :] * inv
+    stores[19].start()
     for store in stores:
         store.wait()
 
@@ -524,25 +531,34 @@
     n_gz, n_gy, n_x, n_z, n_core = sizes
     names = scratch_list(rows, cols, (n_core * n_gy - 1, n_z - 1, n_x - 1))
     f32 = jnp.float32
-    anywhere = pl.BlockSpec(memory_space=pl.ANY)
+    in_hbm = pl.BlockSpec(memory_space=pltpu.HBM)
+    in_vmem = pl.BlockSpec(memory_space=pltpu.VMEM)
+    lam_type = jax.ShapeDtypeStruct(populations.shape, f32)
+    sens_type = jax.ShapeDtypeStruct(solid_fraction.shape, f32)
+    limit = 24 * 1024 * 1024
     lam, sens, total = pl.pallas_call(
         functools.partial(kernel, tuple(names), sizes),
-        out_shape=(
-            jax.ShapeDtypeStruct(populations.shape, f32),
-            jax.ShapeDtypeStruct(solid_fraction.shape, f32),
-            jax.ShapeDtypeStruct((8, 128), f32),
-        ),
-        in_specs=[anywhere] * 3,
-        out_specs=(anywhere,) * 3,
+        out_shape=(lam_type, sens_type, jax.ShapeDtypeStruct((ROWS, cols), f32)),
+        in_specs=[in_hbm] * 3,
+        out_specs=(in_vmem,) * 3,
         scratch_shapes=list(names.values()),
-        compiler_params=pltpu.CompilerParams(
-            collective_id=0, has_side_effects=True, vmem_limit_bytes=24 * 1024 * 1024
-        ),
+        compiler_params=pltpu.CompilerParams(collective_id=0, has_side_effects=True, vmem_limit_bytes=limit),
         name="lattice",
-    )(populations, solid_fraction, labels)
-    cells = n_gz * n_gy * rows * cols
-    mean_energy = total[0, 0] / (STEPS * cells)
-    return (sens / mean_energy, lam / mean_energy)
+    )(*[pltpu.with_memory_space_constraint(v, pltpu.HBM) for v in (populations, solid_fraction, labels)])
+    scale = 1.0 / (STEPS * n_gz * n_gy * rows * cols)
+    return pl.pallas_call(
+        functools.partial(finish, scale),
+        out_shape=(sens_type, lam_type),
+        in_specs=[in_vmem] * 3,
+        out_specs=(in_hbm,) * 2,
+        scratch_shapes=[
+            pltpu.VMEM(populations.shape, f32),
+            pltpu.VMEM(solid_fraction.shape, f32),
+            pltpu.SemaphoreType.DMA((20,)),
+        ],
+        compiler_params=pltpu.CompilerParams(vmem_limit_bytes=4 * 1024 * 1024),
+        name="finish",
+    )(lam, sens, total)
 
 
 def solution(mesh):

time: 43.1 us -> 34.9 us (0.81)
  the two profiles are of different devices: /device:TPU:0 before, /device:TPU:8 now
where the time goes in v2:
time: 34.9 us; the launch traced here: 34.8 us
  Pallas kernels  34.2 us (98%)
  between operations  0.64 us (2%)
    pallas_call x1, Pallas kernels, on_device(): pl.pallas_call(functools.partial(kernel, tuple(names), sizes), out_shape=...  33.2 us
    pallas_call x1, Pallas kernels, on_device(): pl.pallas_call(functools.partial(finish, scale), out_shape=(sens_type, la...  1.01 us

profile of v2, /device:TPU:8, one launch (start us, length us, event | category | flops | bytes accessed | tf_op | source)
XLA Modules:
  0.0 34.8 jit_solution(16851565138417681734)
XLA Ops:
  0.6 33.2 %lattice.1 = (f32[19,1,32,256]{3,2,1,0:T(8,128)S(1)}, f32[1,32,256]{2,1,0:T(8,128)S(1)}, f32[8,256]{1,0:T(8,128)S(1)}) custom-call(f32[19,1,32,256]{3,2,1,0:T(8,128)} %pop_ref.1, f32[1,32,256]{2,1,0:T(8,128)} %sol_ref.1, s32[1,32,256]{2,1,0:T(8,128)} %lab_ref.1), custom_call_target="tpu_custom_call" | custom-call | tf_op jit(solution)/shard_map/lattice/pallas_call | solution.py:539
  33.8 1.0 %finish.1 = (f32[1,32,256]{2,1,0:T(8,128)}, f32[19,1,32,256]{3,2,1,0:T(8,128)}) custom-call(f32[19,1,32,256]{3,2,1,0:T(8,128)S(1)} %get-tuple-element.5.lam_ref, f32[1,32,256]{2,1,0:T(8,128)S(1)} %get-tuple-element.6.sens_ref, f32[8,256]{1,0:T(8,128)S(1)} %get-tuple-element.7.en_ref), custom_call_target="tpu_custom_call" | custom-call | tf_op jit(solution)/shard_map/finish/pallas_call | solution.py:549

commit v3 on v2

--- a/solution.py
+++ b/solution.py
@@ -205,9 +205,8 @@
         return ((x * n_z + z) * n_core + c, lax.rem(gy + dy, n_gy))
 
     stages = [
-        [place(0, 0, dc, dy) for dc in range(n_core) for dy in range(n_gy) if (dc, dy) != (0, 0)],
-        [place(0, dz, 0, 0) for dz in range(1, n_z)],
-        [place(dx, 0, 0, 0) for dx in range(1, n_x)],
+        [place(0, dz, dc, 0) for dz in range(n_z) for dc in range(n_core) if (dz, dc) != (0, 0)],
+        [place(dx, 0, 0, dy) for dx in range(n_x) for dy in range(n_gy) if (dx, dy) != (0, 0)],
     ]
     near = [at(dz, dy) for dz, dy in ((1, 0), (-1, 0), (0, 1), (0, -1), (1, 1), (1, -1), (-1, 1), (-1, -1))]
     barrier = pltpu.get_barrier_semaphore()
@@ -225,9 +224,9 @@
             device_id_type=MESH,
         )
         copy.start()
-        started[r].append(copy)
-
-    started = [[], [], [], []]
+        started[r][i] = copy
+
+    started = [{}, {}, {}, {}]
 
     def send_bulk(r, k):
         src, dst = pl.ds(k * ROWS, ROWS), pl.ds(TOP + k * ROWS, ROWS)
@@ -246,9 +245,22 @@
             send_edges(r)
         send_bulk(r, k)
 
-    def receive(r):
-        for copy in started[r]:
-            copy.wait_recv()
+    landed = set()
+
+    def receive_part(r, i):
+        if (r, i) not in landed:
+            landed.add((r, i))
+            started[r][i].wait_recv()
+
+    def receive(r, k):
+        for j in (k - 1, k, k + 1):
+            if 0 <= j < chunks:
+                receive_part(r, j)
+                receive_part(r, chunks + j)
+        first = (r, 2 * chunks) not in landed
+        for i in range(6):
+            receive_part(r, 2 * chunks + i)
+        return first
 
     def interior(k):
         return pl.ds(TOP + k * ROWS, ROWS)
@@ -304,7 +316,6 @@
 
     for load in loads:
         load.wait()
-    pl.semaphore_wait(barrier, len(greeted))
     for k in order:
         here = pl.ds(k * ROWS, ROWS)
         label = S["lab"][0, here, :]
@@ -319,12 +330,16 @@
         for i, value in enumerate((rho, *u)):
             S["mom0"][i, here, :] = value
         emit_populations(0, k, post, 1)
-        send_chunk(0, k)
-
-    receive(0)
-    place_edges(0)
+
+    pl.semaphore_wait(barrier, len(greeted))
+    send_edges(0)
     for k in order:
-        here = pl.ds(k * ROWS, ROWS)
+        send_bulk(0, k)
+
+    for k in order:
+        here = pl.ds(k * ROWS, ROWS)
+        if receive(0, k):
+            place_edges(0)
         a, b, s = coefficients(k)
         f = gather_populations(0, k, 1)
         for q in range(19):
@@ -364,14 +379,17 @@
                 S["yd1"][1:2, :] = along[:1, :]
         send_chunk(1, k)
 
-    receive(1)
-    for i, name, row in ((0, "rup1", TOP - 1), (1, "rup1", last), (2, "rdn1", TOP - 1), (3, "rdn1", last)):
-        S[name][2 + i % 2, pl.ds(row, 1), :] = S[f"rdg1{i}"][...]
-    for j in range(2):
-        S["part"][2 + j, pl.ds(TOP - 1, 1), :] = S["ryu1"][j : j + 1, :]
-        S["part"][4 + j, pl.ds(last, 1), :] = S["ryd1"][j : j + 1, :]
+    def place_moments():
+        for i, name, row in ((0, "rup1", TOP - 1), (1, "rup1", last), (2, "rdn1", TOP - 1), (3, "rdn1", last)):
+            S[name][2 + i % 2, pl.ds(row, 1), :] = S[f"rdg1{i}"][...]
+        for j in range(2):
+            S["part"][2 + j, pl.ds(TOP - 1, 1), :] = S["ryu1"][j : j + 1, :]
+            S["part"][4 + j, pl.ds(last, 1), :] = S["ryd1"][j : j + 1, :]
+
     for k in order:
         here = pl.ds(k * ROWS, ROWS)
+        if receive(1, k):
+            place_moments()
         s = S["coef"][2, here, :]
         above, below = {}, {}
         for table, name in ((above, "rup1"), (below, "rdn1")):
@@ -442,17 +460,21 @@
     reduce_send(0, jnp.sum(acc, axis=0, keepdims=True))
 
     zero_row = jnp.zeros((1, cols), jnp.float32)
-    reduce_send(1, reduce_receive(0))
-    receive(2)
-    for i, name, row in ((0, "rup2", TOP - 1), (1, "rup2", last), (2, "rdn2", TOP - 1), (3, "rdn2", last)):
-        S[name][2, pl.ds(row, 1), :] = S[f"rdg2{i}"][...]
-        S[name][1, pl.ds(row, 1), :] = zero_row
-    for j, slot in ((0, 0), (1, 2)):
-        S["grad"][slot, pl.ds(TOP - 1, 1), :] = S["ryu2"][j : j + 1, :]
-    for j, slot in ((0, 0), (1, 1)):
-        S["grad"][slot, pl.ds(last, 1), :] = S["ryd2"][j : j + 1, :]
+    def place_gradients():
+        for i, name, row in ((0, "rup2", TOP - 1), (1, "rup2", last), (2, "rdn2", TOP - 1), (3, "rdn2", last)):
+            S[name][2, pl.ds(row, 1), :] = S[f"rdg2{i}"][...]
+            S[name][1, pl.ds(row, 1), :] = zero_row
+        for j, slot in ((0, 0), (1, 2)):
+            S["grad"][slot, pl.ds(TOP - 1, 1), :] = S["ryu2"][j : j + 1, :]
+        for j, slot in ((0, 0), (1, 1)):
+            S["grad"][slot, pl.ds(last, 1), :] = S["ryd2"][j : j + 1, :]
+
     for k in order:
         here = pl.ds(k * ROWS, ROWS)
+        if receive(2, k):
+            place_gradients()
+        if k == order[1]:
+            reduce_send(1, reduce_receive(0))
         a, b, s = coefficients(k)
         mu = [None] * 19
         for name, cz in (("rup2", -1), ("rdn2", 1)):
@@ -484,11 +506,10 @@
         emit_populations(3, k, lam, -1)
         send_chunk(3, k)
 
-    reduce_send(2, reduce_receive(1))
-    receive(3)
-    place_edges(3)
     for k in order:
         here = pl.ds(k * ROWS, ROWS)
+        if receive(3, k):
+            place_edges(3)
         a, b, s = coefficients(k)
         mu = gather_populations(3, k, -1)
         f = [S["f0"][q, 0, here, :] for q in range(19)]
@@ -498,10 +519,10 @@
         for q in range(19):
             lam_ref[q, 0, here, :] = lam[q]
         sens_ref[0, here, :] = jnp.where(S["lab"][0, here, :] == 1, S["ds"][here, :] + by_s, 0.0)
-    total = jnp.sum(reduce_receive(2), axis=1, keepdims=True)
+    total = jnp.sum(reduce_receive(1), axis=1, keepdims=True)
     en_ref[...] = jnp.broadcast_to(total, en_ref.shape)
     for copies in started:
-        for copy in copies:
+        for copy in copies.values():
             copy.wait_send()
     for stage, copy in sums:
         copy.wait_send()
@@ -529,7 +550,7 @@
 def on_device(sizes, populations, solid_fraction, labels):
     rows, cols = solid_fraction.shape[1:]
     n_gz, n_gy, n_x, n_z, n_core = sizes
-    names = scratch_list(rows, cols, (n_core * n_gy - 1, n_z - 1, n_x - 1))
+    names = scratch_list(rows, cols, (n_core * n_z - 1, n_x * n_gy - 1))
     f32 = jnp.float32
     in_hbm = pl.BlockSpec(memory_space=pltpu.HBM)
     in_vmem = pl.BlockSpec(memory_space=pltpu.VMEM)

time: 34.9 us -> 34.4 us (0.986)
  Pallas kernels: 34.2 us -> 33.7 us
    pallas_call x1, Pallas kernels: 33.2 us -> 32.7 us  [on_device(): pl.pallas_call(functools.partial(kernel, tuple(names), sizes), out_shape=...]
where the time goes in v3:
time: 34.4 us; the launch traced here: 34.3 us
  Pallas kernels  33.7 us (98%)
  between operations  0.64 us (2%)
    pallas_call x1, Pallas kernels, on_device(): pl.pallas_call(functools.partial(kernel, tuple(names), sizes), out_shape=...  32.7 us
    pallas_call x1, Pallas kernels, on_device(): pl.pallas_call(functools.partial(finish, scale), out_shape=(sens_type, la...  1.01 us

profile of v3, /device:TPU:8, one launch (start us, length us, event | category | flops | bytes accessed | tf_op | source)
XLA Modules:
  0.0 34.3 jit_solution(366818911197422879)
XLA Ops:
  0.6 32.7 %lattice.1 = (f32[19,1,32,256]{3,2,1,0:T(8,128)S(1)}, f32[1,32,256]{2,1,0:T(8,128)S(1)}, f32[8,256]{1,0:T(8,128)S(1)}) custom-call(f32[19,1,32,256]{3,2,1,0:T(8,128)} %pop_ref.1, f32[1,32,256]{2,1,0:T(8,128)} %sol_ref.1, s32[1,32,256]{2,1,0:T(8,128)} %lab_ref.1), custom_call_target="tpu_custom_call" | custom-call | tf_op jit(solution)/shard_map/lattice/pallas_call | solution.py:560
  33.3 1.0 %finish.1 = (f32[1,32,256]{2,1,0:T(8,128)}, f32[19,1,32,256]{3,2,1,0:T(8,128)}) custom-call(f32[19,1,32,256]{3,2,1,0:T(8,128)S(1)} %get-tuple-element.5.lam_ref, f32[1,32,256]{2,1,0:T(8,128)S(1)} %get-tuple-element.6.sens_ref, f32[8,256]{1,0:T(8,128)S(1)} %get-tuple-element.7.en_ref), custom_call_target="tpu_custom_call" | custom-call | tf_op jit(solution)/shard_map/finish/pallas_call | solution.py:570

commit v4 on v3

v4 whole, which is shorter than its diff:
```python
import functools
import types

import jax
import jax.numpy as jnp
from jax import lax
from jax.experimental import pallas as pl
from jax.experimental.pallas import tpu as pltpu
from jax.sharding import PartitionSpec as P

STEPS = 2
OMEGA = 0.9
INLET_SPEED = 0.05
ROWS = 8
TOP = 8
MESH = pl.DeviceIdType.MESH
LANES = 128
EDGE_ROWS = ((0, 4), (1, 8), (2, 2), (3, 4))
GROUPS = [(r, g) for r in (0, 2, 3, 4) for g in ("A", "B", "E")]
GROUPS += [(1, side + g) for side in ("f", "n") for g in ("A", "B", "E")] + [(5, "A"), (6, "A"), (7, "A")]


def velocity_table():
    velocities = [(0, 0, 0)]
    for axis in range(3):
        for sign in (1, -1):
            vector = [0, 0, 0]
            vector[axis] = sign
            velocities.append(tuple(vector))
    for first in range(3):
        for second in range(first + 1, 3):
            for sign_a in (1, -1):
                for sign_b in (1, -1):
                    vector = [0, 0, 0]
                    vector[first] = sign_a
                    vector[second] = sign_b
                    velocities.append(tuple(vector))
    weights = [1.0 / 3.0] + [1.0 / 18.0] * 6 + [1.0 / 36.0] * 12
    opposite = [velocities.index(tuple((-e for e in vector))) for vector in velocities]
    return (velocities, weights, opposite)


VEL, WEIGHT, OPP = velocity_table()
INDEX = {v: q for q, v in enumerate(VEL)}
PAIRS = [(q, OPP[q]) for q in range(19) if q < OPP[q]]
UP = [(0, 0, 1), (1, 0, 1), (-1, 0, 1), (0, 1, 1), (0, -1, 1)]
DOWN = [(0, 0, -1), (1, 0, -1), (-1, 0, -1), (0, 1, -1), (0, -1, -1)]
FLAT = [v for v in VEL if v[2] == 0]
FLAT_UP = [(0, 1, 0), (1, 1, 0), (-1, 1, 0)]
FLAT_DOWN = [(0, -1, 0), (1, -1, 0), (-1, -1, 0)]


def inlet_value(q):
    along = VEL[q][2] * INLET_SPEED
    return WEIGHT[q] * (1.0 + 3.0 * along + 4.5 * along * along - 1.5 * INLET_SPEED * INLET_SPEED)


def roll_x(value, shift):
    if shift == 0:
        return value
    return pltpu.roll(value, shift % value.shape[1], 1)


def signed(terms):
    total = None
    for sign, value in terms:
        if sign == 0:
            continue
        if total is None:
            total = value if sign > 0 else -value
        else:
            total = total + value if sign > 0 else total - value
    return total


def dot_c(c, vector):
    return signed([(c[i], vector[i]) for i in range(3)])


def collide(f, a, b, s, k):
    rho = functools.reduce(lambda p, q: p + q, f)
    m = [signed([(VEL[q][i], f[q]) for q in range(19)]) for i in range(3)]
    inv = 1.0 / rho
    u = [m[i] * inv for i in range(3)]
    speed = u[0] * u[0] + u[1] * u[1] + u[2] * u[2]
    brho = b * rho
    base = brho * (1.0 - 1.5 * speed)
    post = [None] * 19
    post[0] = (a + s) * f[0] + WEIGHT[0] * base + k * inlet_value(0)
    for q, o in PAIRS:
        w = WEIGHT[q]
        along = dot_c(VEL[q], u)
        even = w * base + (4.5 * w) * (brho * along) * along
        odd = (3.0 * w) * (brho * along)
        post[q] = a * f[q] + s * f[o] + (even + odd) + k * inlet_value(q)
        post[o] = a * f[o] + s * f[q] + (even - odd) + k * inlet_value(o)
    return rho, u, speed, post


def collide_adjoint(mu, f, rho, u, speed, a, b, s):
    plus = {q: mu[q] + mu[o] for q, o in PAIRS}
    minus = {q: mu[q] - mu[o] for q, o in PAIRS}

    def weighted(table, first, second=None):
        axial, diagonal = [], []
        for q, o in PAIRS:
            c = VEL[q]
            sign = c[first] if second is None else c[first] * c[second]
            (axial if WEIGHT[q] == WEIGHT[1] else diagonal).append((sign, table[q]))
        one, two = signed(axial), signed(diagonal)
        two = two * WEIGHT[7]
        return two if one is None else one * WEIGHT[1] + two

    axial = functools.reduce(lambda p, q: p + q, [plus[q] for q, o in PAIRS if WEIGHT[q] == WEIGHT[1]])
    diagonal = functools.reduce(lambda p, q: p + q, [plus[q] for q, o in PAIRS if WEIGHT[q] != WEIGHT[1]])
    big_a = WEIGHT[0] * mu[0] + WEIGHT[1] * axial + WEIGHT[7] * diagonal
    big_b = [3.0 * weighted(minus, i) for i in range(3)]
    big_c = {}
    for i in range(3):
        for j in range(i, 3):
            big_c[i, j] = big_c[j, i] = 4.5 * weighted(plus, i, j)
    cu = [sum(big_c[i, j] * u[j] for j in range(3)) for i in range(3)]
    quad = cu[0] * u[0] + cu[1] * u[1] + cu[2] * u[2] - 1.5 * speed * big_a
    by_rho = b * (big_a - quad)
    by_m = [b * (big_b[i] + 2.0 * cu[i] - 3.0 * big_a * u[i]) for i in range(3)]
    lam = [None] * 19
    lam[0] = (a + s) * mu[0] + by_rho
    same = mu[0] * f[0]
    cross = same
    for q, o in PAIRS:
        along = dot_c(VEL[q], by_m)
        lam[q] = a * mu[q] + s * mu[o] + (by_rho + along)
        lam[o] = a * mu[o] + s * mu[q] + (by_rho - along)
        same = same + (mu[q] * f[q] + mu[o] * f[o])
        cross = cross + (mu[q] * f[o] + mu[o] * f[q])
    total = rho * (big_a + big_b[0] * u[0] + big_b[1] * u[1] + big_b[2] * u[2] + quad)
    by_s = cross - ((1.0 - OMEGA) * same + OMEGA * total)
    return lam, by_s


def scratch_tree(rows, cols, n_ar):
    def vmem(*shape):
        return pltpu.VMEM(shape, jnp.float32)

    padded = rows + 16
    dma = pltpu.SemaphoreType.DMA
    return dict(
        f0=vmem(19, 1, rows, cols),
        sol=vmem(1, rows, cols),
        lab=pltpu.VMEM((1, rows, cols), jnp.int32),
        coef=vmem(3, rows, cols),
        mom0=vmem(4, rows, cols),
        mom1=vmem(4, rows, cols),
        f1=vmem(19, rows, cols),
        ds=vmem(rows, cols),
        acc=vmem(ROWS, cols),
        in_sem=dma((1,)),
        ssem=dma((8,)),
        rsem=dma((len(GROUPS),)),
        some=vmem(3 * 19 * rows * cols // LANES, 1, LANES),
        part=vmem(6, padded, cols),
        grad=vmem(4, padded, cols),
        out1=vmem(2, 4, padded, cols),
        in1=vmem(2, 4, padded, cols),
        side=vmem(2, 3, padded, cols),
        mine=vmem(3, rows, cols),
        rest=vmem(4, rows, cols),
        far_rest=vmem(4, rows, cols),
        far_s=vmem(rows, cols),
        s_hi=vmem(1, cols),
        s_lo=vmem(1, cols),
        far_s_hi=vmem(1, cols),
        far_s_lo=vmem(1, cols),
        rest_hi=vmem(4, cols),
        rest_lo=vmem(4, cols),
        far_rest_hi=vmem(4, cols),
        far_rest_lo=vmem(4, cols),
        yu={r: vmem(n, cols) for r, n in EDGE_ROWS},
        yd={r: vmem(n, cols) for r, n in EDGE_ROWS},
        ryu={r: vmem(n, cols) for r, n in EDGE_ROWS},
        ryd={r: vmem(n, cols) for r, n in EDGE_ROWS},
        up={r: vmem(5, rows, cols) for r in (0, 3)},
        dn={r: vmem(5, rows, cols) for r in (0, 3)},
        rup={r: vmem(5, padded, cols) for r in (0, 3)},
        rdn={r: vmem(5, padded, cols) for r in (0, 3)},
        flat={r: vmem(9, padded, cols) for r in (0, 3)},
        dg=[[vmem(1, cols) for i in range(4)] for r in range(4)],
        rdg=[[vmem(1, cols) for i in range(4)] for r in range(4)],
        ar=[vmem(1, LANES) for count in n_ar],
        arr=[[vmem(1, LANES) for i in range(count)] for count in n_ar],
    )


def kernel(tree, sizes, pop_ref, sol_ref, lab_ref, lam_ref, sens_ref, en_ref, *refs):
    S = types.SimpleNamespace(**jax.tree.unflatten(tree, refs))
    n_gz, n_gy, n_x, n_z, n_core = sizes
    rows, cols = S.ds.shape
    chunks = rows // ROWS
    order = [0, chunks - 1, *range(1, chunks - 1)]
    last = TOP + rows
    gz = lax.axis_index("gz")
    gy = lax.axis_index("gy")

    def size(ref):
        return functools.reduce(lambda p, q: p * q, ref.shape) // LANES

    def wait_bytes(count, sem):
        some = S.some.at[pl.ds(0, count)]
        pltpu.make_async_copy(some, some, sem).wait()

    loads = ((pop_ref, S.f0), (sol_ref, S.sol), (lab_ref, S.lab))
    for src, dst in loads:
        pltpu.make_async_copy(src, dst, S.in_sem.at[0]).start()

    def at(dz, dy):
        return (lax.rem(gz + dz + n_gz, n_gz), lax.rem(gy + dy + n_gy, n_gy))

    core = lax.rem(gz, n_core)
    zpos = lax.rem(gz // n_core, n_z)
    xpos = gz // (n_core * n_z)

    def place(dx, dz, dcore, dy):
        x = lax.rem(xpos + dx, n_x)
        z = lax.rem(zpos + dz, n_z)
        c = lax.rem(core + dcore, n_core)
        return ((x * n_z + z) * n_core + c, lax.rem(gy + dy, n_gy))

    stages = [
        [place(0, dz, dc, 0) for dz in range(n_z) for dc in range(n_core) if (dz, dc) != (0, 0)],
        [place(dx, 0, 0, dy) for dx in range(n_x) for dy in range(n_gy) if (dx, dy) != (0, 0)],
    ]
    near = [at(dz, dy) for dz, dy in ((1, 0), (-1, 0), (0, 1), (0, -1), (1, 1), (1, -1), (-1, 1), (-1, -1))]
    barrier = pltpu.get_barrier_semaphore()
    greeted = near + stages[0] + [place(dx, 0, 0, 0) for dx in range(1, n_x)]
    for device in greeted:
        pl.semaphore_signal(barrier, inc=1, device_id=device, device_id_type=MESH)

    sent_bytes, group_bytes = {}, {}

    def group_of(r, i):
        if i >= base:
            name = "E"
        else:
            name = "B" if i % chunks == order[-1] and r != 5 else "A"
        if r == 1:
            near_side = i - base not in (2, 3) if i >= base else i >= chunks
            name = ("n" if near_side else "f") + name
        return (r, name)

    def send(src, dst, r, i, device):
        group = group_of(r, i)
        pltpu.make_async_remote_copy(
            src_ref=src,
            dst_ref=dst,
            send_sem=S.ssem.at[r],
            recv_sem=S.rsem.at[GROUPS.index(group)],
            device_id=device,
            device_id_type=MESH,
        ).start()
        sent_bytes[r] = sent_bytes.get(r, 0) + size(src)
        group_bytes[group] = group_bytes.get(group, 0) + size(src)

    far, near_z = 2 * core - 1, 1 - 2 * core
    upward, downward = 1 - core, core
    base = 2 * chunks
    DIAGONAL = ((1, 1), (1, -1), (-1, 1), (-1, -1))
    FAR_DIAGONAL = ((far, 1), (far, -1), (near_z, 1), (near_z, -1))

    def send_bulk(r, k):
        src, dst = pl.ds(k * ROWS, ROWS), pl.ds(TOP + k * ROWS, ROWS)
        if r in (0, 3):
            send(S.up[r].at[:, src, :], S.rup[r].at[:, dst, :], r, k, at(1, 0))
            send(S.dn[r].at[:, src, :], S.rdn[r].at[:, dst, :], r, chunks + k, at(-1, 0))
        if r == 1:
            send(S.out1.at[1, :, dst, :], S.in1.at[1, :, dst, :], 1, chunks + k, at(near_z, 0))
            send(S.out1.at[0, :, dst, :], S.in1.at[0, :, dst, :], 1, k, at(far, 0))
        if r == 2:
            send(S.mine.at[:, src, :], S.side.at[1, :, dst, :], 2, chunks + k, at(near_z, 0))
        if r == 4:
            send(S.rest.at[:, src, :], S.far_rest.at[:, src, :], 4, k, at(far, 0))

    def send_edges(r):
        if r == 4:
            send(S.rest_hi, S.far_rest_hi, 4, base + 2, at(far, 1))
            send(S.rest_lo, S.far_rest_lo, 4, base + 3, at(far, -1))
            return
        send(S.yu[r], S.ryu[r], r, base, at(0, 1))
        send(S.yd[r], S.ryd[r], r, base + 1, at(0, -1))
        for i, (dz, dy) in enumerate(DIAGONAL if r in (0, 3) else FAR_DIAGONAL):
            if r != 2 or i >= 2:
                send(S.dg[r][i], S.rdg[r][i], r, base + 2 + i, at(dz, dy))

    def send_chunk(r, k):
        if k == chunks - 1:
            send_edges(r)
        send_bulk(r, k)

    def sent(*rounds):
        for r in rounds:
            wait_bytes(sent_bytes[r], S.ssem.at[r])

    landed = set()

    def receive_group(r, name):
        if (r, name) not in landed:
            landed.add((r, name))
            wait_bytes(group_bytes[r, name], S.rsem.at[GROUPS.index((r, name))])

    def receive(r, k, side="", reach=1):
        receive_group(r, side + "A")
        if abs(k - order[-1]) <= reach:
            receive_group(r, side + "B")
        receive_group(r, side + "E")
        return k == order[0]

    def interior(k):
        return pl.ds(TOP + k * ROWS, ROWS)

    def moved(k, dy):
        return pl.ds(TOP + k * ROWS - dy, ROWS)

    def emit_populations(r, k, values, sense):
        here = pl.ds(k * ROWS, ROWS)
        for moving, table in ((S.up, UP), (S.dn, DOWN)):
            for i, d in enumerate(table):
                q = INDEX[tuple(sense * e for e in d)]
                value = roll_x(values[q], d[0])
                moving[r][i, here, :] = value
                slot = DIAGONAL.index((d[2], d[1])) if d[1] else None
                if d[1] == 1 and k == chunks - 1:
                    S.dg[r][slot][...] = value[ROWS - 1 :, :]
                if d[1] == -1 and k == 0:
                    S.dg[r][slot][...] = value[:1, :]
        for i, d in enumerate(FLAT):
            q = INDEX[tuple(sense * e for e in d)]
            value = roll_x(values[q], d[0])
            S.flat[r][i, interior(k), :] = value
            if d[1] == 1 and k == chunks - 1:
                j = FLAT_UP.index(d)
                S.yu[r][j : j + 1, :] = value[ROWS - 1 :, :]
            if d[1] == -1 and k == 0:
                j = FLAT_DOWN.index(d)
                S.yd[r][j : j + 1, :] = value[:1, :]

    def place_edges(r):
        for i, arrived, row in ((0, S.rup, TOP - 1), (1, S.rup, last), (2, S.rdn, TOP - 1), (3, S.rdn, last)):
            slot = 3 if i % 2 == 0 else 4
            arrived[r][slot, pl.ds(row, 1), :] = S.rdg[r][i][...]
        for j in range(3):
            S.flat[r][FLAT.index(FLAT_UP[j]), pl.ds(TOP - 1, 1), :] = S.ryu[r][j : j + 1, :]
            S.flat[r][FLAT.index(FLAT_DOWN[j]), pl.ds(last, 1), :] = S.ryd[r][j : j + 1, :]

    def gather_populations(r, k, sense):
        values = [None] * 19
        for arrived, table in ((S.rup, UP), (S.rdn, DOWN), (S.flat, FLAT)):
            for i, d in enumerate(table):
                q = INDEX[tuple(sense * e for e in d)]
                values[q] = arrived[r][i, moved(k, d[1]), :]
        return values

    def coefficients(k):
        here = pl.ds(k * ROWS, ROWS)
        return [S.coef[i, here, :] for i in range(3)]

    def inlet(k):
        return jnp.where(S.lab[0, pl.ds(k * ROWS, ROWS), :] == 3, 1.0, 0.0)

    wait_bytes(sum(size(dst) for src, dst in loads), S.in_sem.at[0])
    for k in order:
        here = pl.ds(k * ROWS, ROWS)
        label = S.lab[0, here, :]
        s = jnp.where(label == 1, S.sol[0, here, :], jnp.where(label == 2, 1.0, 0.0))
        free = jnp.where(label == 3, 0.0, 1.0 - s)
        b = jnp.where(label == 4, free, OMEGA * free)
        a = jnp.where(label == 4, 0.0, (1.0 - OMEGA) * free)
        for i, value in enumerate((a, b, s)):
            S.coef[i, here, :] = value
        f = [S.f0[q, 0, here, :] for q in range(19)]
        rho, u, speed, post = collide(f, a, b, s, inlet(k))
        for i, value in enumerate((rho, *u)):
            S.mom0[i, here, :] = value
        emit_populations(0, k, post, 1)

    pl.semaphore_wait(barrier, len(greeted))
    send_edges(0)
    for k in order:
        send_bulk(0, k)
    S.s_hi[...] = S.coef[2, pl.ds(rows - 1, 1), :]
    S.s_lo[...] = S.coef[2, pl.ds(0, 1), :]
    send(S.s_hi, S.far_s_hi, 5, 1, at(far, 1))
    send(S.s_lo, S.far_s_lo, 5, 2, at(far, -1))
    send(S.coef.at[2], S.far_s, 5, 0, at(far, 0))

    for k in order:
        here = pl.ds(k * ROWS, ROWS)
        if receive(0, k):
            place_edges(0)
        a, b, s = coefficients(k)
        f = gather_populations(0, k, 1)
        for q in range(19):
            S.f1[q, here, :] = f[q]
        rho, u, speed, post = collide(f, a, b, s, inlet(k))
        for i, value in enumerate((rho, *u)):
            S.mom1[i, here, :] = value
        flow = rho * speed
        S.ds[here, :] = -flow
        energy = (1.0 - s) * flow
        S.acc[...] = energy if k == 0 else S.acc[...] + energy

        def three(cy, cz):
            mid = post[INDEX[0, cy, cz]]
            right = roll_x(post[INDEX[1, cy, cz]], 1)
            left = roll_x(post[INDEX[-1, cy, cz]], -1)
            return mid + right + left, right - left

        for slot, cz in ((upward, 1), (downward, -1)):
            total, along = three(0, cz)
            for i, value in enumerate((total, along, post[INDEX[0, 1, cz]], post[INDEX[0, -1, cz]])):
                S.out1[slot, i, interior(k), :] = value
        if k == chunks - 1:
            end = pl.ds(last - 1, 1)
            for j, (i, row) in enumerate(((0, end), (1, end), (2, pl.ds(last - 2, 1)), (2, end))):
                S.yu[1][2 + j : 3 + j, :] = S.out1[0, i, row, :]
            S.dg[1][0][...] = S.out1[0, 2, end, :]
            S.dg[1][2][...] = S.out1[1, 2, end, :]
        if k == 0:
            end = pl.ds(TOP, 1)
            for j, (i, row) in enumerate(((0, end), (1, end), (3, pl.ds(TOP + 1, 1)), (3, end))):
                S.yd[1][2 + j : 3 + j, :] = S.out1[0, i, row, :]
            S.dg[1][1][...] = S.out1[0, 3, end, :]
            S.dg[1][3][...] = S.out1[1, 3, end, :]
        for j, cy in enumerate((0, 1, -1)):
            total, along = three(cy, 0)
            S.part[2 * j, interior(k), :] = total
            S.part[2 * j + 1, interior(k), :] = along
            if cy == 1 and k == chunks - 1:
                S.yu[1][0:1, :] = total[ROWS - 1 :, :]
                S.yu[1][1:2, :] = along[ROWS - 1 :, :]
            if cy == -1 and k == 0:
                S.yd[1][0:1, :] = total[:1, :]
                S.yd[1][1:2, :] = along[:1, :]
        send_chunk(1, k)

    sent(0, 5)

    def place_halo(side, i):
        S.in1[side, 2, pl.ds(TOP - 1, 1), :] = S.rdg[1][i][...]
        S.in1[side, 3, pl.ds(last, 1), :] = S.rdg[1][i + 1][...]

    for k in order:
        here = pl.ds(k * ROWS, ROWS)
        if receive(1, k, "n"):
            place_halo(1, 2)
            for j in range(2):
                S.part[2 + j, pl.ds(TOP - 1, 1), :] = S.ryu[1][j : j + 1, :]
                S.part[4 + j, pl.ds(last, 1), :] = S.ryd[1][j : j + 1, :]
            S.out1[0, 2, pl.ds(TOP - 1, 1), :] = S.ryu[1][5:6, :]
            S.out1[0, 3, pl.ds(last, 1), :] = S.ryd[1][5:6, :]
        near_x = S.in1[1, 1, interior(k), :]
        near_a, near_b = S.in1[1, 2, moved(k, 1), :], S.in1[1, 3, moved(k, -1), :]
        mass = S.in1[1, 0, interior(k), :] + (near_a + near_b)
        mid, mid_x = S.part[0, interior(k), :], S.part[1, interior(k), :]
        ahead, ahead_x = S.part[2, moved(k, 1), :], S.part[3, moved(k, 1), :]
        behind, behind_x = S.part[4, moved(k, -1), :], S.part[5, moved(k, -1), :]
        rest = (
            mass + (mid + (ahead + behind)),
            near_x + (mid_x + (ahead_x + behind_x)),
            (near_a - near_b) + (ahead - behind),
            mass,
        )
        for i, value in enumerate(rest):
            S.rest[i, here, :] = value
            if k == chunks - 1:
                S.rest_hi[i : i + 1, :] = value[ROWS - 1 :, :]
            if k == 0:
                S.rest_lo[i : i + 1, :] = value[:1, :]
        send_chunk(4, k)

    def finish_moments(rest, total, along, ahead, behind, s):
        mass = total + (ahead + behind)
        rho = rest[0] + mass
        inv = 1.0 / rho
        u = [(rest[1] + along) * inv, (rest[2] + (ahead - behind)) * inv, (mass - rest[3]) * inv]
        speed = u[0] * u[0] + u[1] * u[1] + u[2] * u[2]
        free = 1.0 - s
        twice = 2.0 * free
        return rho, speed, [twice * v for v in u], free

    for k in order:
        here = pl.ds(k * ROWS, ROWS)
        if receive(1, k, "f"):
            place_halo(0, 0)
        rho, speed, (x, y, z), free = finish_moments(
            [S.rest[i, here, :] for i in range(4)],
            S.in1[0, 0, interior(k), :],
            S.in1[0, 1, interior(k), :],
            S.in1[0, 2, moved(k, 1), :],
            S.in1[0, 3, moved(k, -1), :],
            S.coef[2, here, :],
        )
        flow = rho * speed
        S.ds[here, :] = S.ds[here, :] - flow
        S.acc[...] = S.acc[...] + free * flow
        e = free * speed
        w = -z - e
        for i, value in enumerate((x, y, w)):
            S.mine[i, here, :] = value
        for i, value in enumerate((x, y - e, -y - e, e)):
            S.grad[i, interior(k), :] = value
        if k == chunks - 1:
            S.dg[2][2][...] = (w - y)[ROWS - 1 :, :]
            S.yu[2][0:1, :] = x[ROWS - 1 :, :]
            S.yu[2][1:2, :] = (-y - e)[ROWS - 1 :, :]
        if k == 0:
            S.dg[2][3][...] = (w + y)[:1, :]
            S.yd[2][0:1, :] = x[:1, :]
            S.yd[2][1:2, :] = (y - e)[:1, :]
        send_chunk(2, k)

    def reduce_send(stage, value):
        S.ar[stage][...] = value
        for i, device in enumerate(stages[stage]):
            pltpu.make_async_remote_copy(
                src_ref=S.ar[stage],
                dst_ref=S.arr[stage][i],
                send_sem=S.ssem.at[6 + stage],
                recv_sem=S.rsem.at[GROUPS.index((6 + stage, "A"))],
                device_id=device,
                device_id_type=MESH,
            ).start()
        sent_bytes[6 + stage] = len(stages[stage])

    def reduce_receive(stage):
        wait_bytes(len(stages[stage]), S.rsem.at[GROUPS.index((6 + stage, "A"))])
        value = S.ar[stage][...]
        for i in range(len(stages[stage])):
            value = value + S.arr[stage][i][...]
        return value

    acc = S.acc[...]
    acc = functools.reduce(lambda p, q: p + q, [acc[:, i : i + 128] for i in range(0, cols, 128)])
    reduce_send(0, jnp.sum(acc, axis=0, keepdims=True))

    zero_row = jnp.zeros((1, cols), jnp.float32)
    sent(1)

    def far_plane(rest, total, along, ahead, behind, s):
        rho, speed, (x, y, z), free = finish_moments(rest, total, along, ahead, behind, s)
        return x, y, z - free * speed

    for k in order:
        here = pl.ds(k * ROWS, ROWS)
        receive_group(5, "A")
        if receive(4, k, "", 0):
            low, high = pl.ds(TOP - 1, 1), pl.ds(last, 1)
            x, y, w = far_plane(
                [S.far_rest_hi[i : i + 1, :] for i in range(4)],
                S.ryu[1][2:3, :],
                S.ryu[1][3:4, :],
                S.ryu[1][4:5, :],
                S.out1[0, 3, pl.ds(TOP, 1), :],
                S.far_s_hi[...],
            )
            S.side[0, 1, low, :] = y
            S.side[0, 2, low, :] = w
            x, y, w = far_plane(
                [S.far_rest_lo[i : i + 1, :] for i in range(4)],
                S.ryd[1][2:3, :],
                S.ryd[1][3:4, :],
                S.out1[0, 2, pl.ds(last - 1, 1), :],
                S.ryd[1][4:5, :],
                S.far_s_lo[...],
            )
            S.side[0, 1, high, :] = y
            S.side[0, 2, high, :] = w
        value = far_plane(
            [S.far_rest[i, here, :] for i in range(4)],
            S.out1[0, 0, interior(k), :],
            S.out1[0, 1, interior(k), :],
            S.out1[0, 2, moved(k, 1), :],
            S.out1[0, 3, moved(k, -1), :],
            S.far_s[here, :],
        )
        for i in range(3):
            S.side[0, i, interior(k), :] = value[i]

    for k in order:
        here = pl.ds(k * ROWS, ROWS)
        if receive(2, k):
            for i, row in ((2, TOP - 1), (3, last)):
                S.side[1, 2, pl.ds(row, 1), :] = S.rdg[2][i][...]
                S.side[1, 1, pl.ds(row, 1), :] = zero_row
            for j, slot in ((0, 0), (1, 2)):
                S.grad[slot, pl.ds(TOP - 1, 1), :] = S.ryu[2][j : j + 1, :]
            for j, slot in ((0, 0), (1, 1)):
                S.grad[slot, pl.ds(last, 1), :] = S.ryd[2][j : j + 1, :]
        a, b, s = coefficients(k)
        mu = [None] * 19
        for slot, cz in ((upward, 1), (downward, -1)):
            x, w = S.side[slot, 0, interior(k), :], S.side[slot, 2, interior(k), :]
            mu[INDEX[0, 0, cz]] = w
            mu[INDEX[1, 0, cz]] = roll_x(w + x, -1)
            mu[INDEX[-1, 0, cz]] = roll_x(w - x, 1)
            mu[INDEX[0, 1, cz]] = S.side[slot, 2, moved(k, -1), :] + S.side[slot, 1, moved(k, -1), :]
            mu[INDEX[0, -1, cz]] = S.side[slot, 2, moved(k, 1), :] - S.side[slot, 1, moved(k, 1), :]
        for cy, slot in ((0, 3), (1, 1), (-1, 2)):
            x, w = S.grad[0, moved(k, -cy), :], S.grad[slot, moved(k, -cy), :]
            w = -w if cy == 0 else w
            mu[INDEX[0, cy, 0]] = w
            mu[INDEX[1, cy, 0]] = roll_x(w + x, -1)
            mu[INDEX[-1, cy, 0]] = roll_x(w - x, 1)
        f = [S.f1[q, here, :] for q in range(19)]
        rho, u = S.mom1[0, here, :], [S.mom1[i, here, :] for i in (1, 2, 3)]
        speed = u[0] * u[0] + u[1] * u[1] + u[2] * u[2]
        lam, by_s = collide_adjoint(mu, f, rho, u, speed, a, b, s)
        S.ds[here, :] = S.ds[here, :] + by_s
        twice = 2.0 * (1.0 - s)
        twice_u = [twice * u[i] for i in range(3)]
        e = (1.0 - s) * speed
        lam[0] = lam[0] - e
        for q, o in PAIRS:
            along = dot_c(VEL[q], twice_u)
            lam[q] = lam[q] + (along - e)
            lam[o] = lam[o] - (along + e)
        emit_populations(3, k, lam, -1)
        send_chunk(3, k)

    reduce_send(1, reduce_receive(0))
    sent(4, 2, 3, 6, 7)

    for k in order:
        here = pl.ds(k * ROWS, ROWS)
        if receive(3, k):
            place_edges(3)
        a, b, s = coefficients(k)
        mu = gather_populations(3, k, -1)
        f = [S.f0[q, 0, here, :] for q in range(19)]
        rho, u = S.mom0[0, here, :], [S.mom0[i, here, :] for i in (1, 2, 3)]
        speed = u[0] * u[0] + u[1] * u[1] + u[2] * u[2]
        lam, by_s = collide_adjoint(mu, f, rho, u, speed, a, b, s)
        for q in range(19):
            lam_ref[q, 0, here, :] = lam[q]
        sens_ref[0, here, :] = jnp.where(S.lab[0, here, :] == 1, S.ds[here, :] + by_s, 0.0)
    total = jnp.sum(reduce_receive(1), axis=1, keepdims=True)
    en_ref[...] = jnp.broadcast_to(total, en_ref.shape)


def finish(scale, lam_ref, sens_ref, en_ref, out_sens, out_lam, lam, sens, some, sems):
    inv = 1.0 / (en_ref[...] * scale)
    rows = sens.shape[1]
    for q in range(19):
        for k in range(rows // ROWS):
            here = pl.ds(k * ROWS, ROWS)
            lam[q, 0, here, :] = lam_ref[q, 0, here, :] * inv
        pltpu.make_async_copy(lam.at[pl.ds(q, 1)], out_lam.at[pl.ds(q, 1)], sems.at[0]).start()
    for k in range(rows // ROWS):
        here = pl.ds(k * ROWS, ROWS)
        sens[0, here, :] = sens_ref[0, here, :] * inv
    pltpu.make_async_copy(sens, out_sens, sems.at[0]).start()
    pltpu.make_async_copy(some, some, sems.at[0]).wait()


def on_device(sizes, populations, solid_fraction, labels):
    rows, cols = solid_fraction.shape[1:]
    n_gz, n_gy, n_x, n_z, n_core = sizes
    leaves, tree = jax.tree.flatten(scratch_tree(rows, cols, (n_core * n_z - 1, n_x * n_gy - 1)))
    f32 = jnp.float32
    in_hbm = pl.BlockSpec(memory_space=pltpu.HBM)
    in_vmem = pl.BlockSpec(memory_space=pltpu.VMEM)
    lam_type = jax.ShapeDtypeStruct(populations.shape, f32)
    sens_type = jax.ShapeDtypeStruct(solid_fraction.shape, f32)
    limit = 24 * 1024 * 1024
    lam, sens, total = pl.pallas_call(
        functools.partial(kernel, tree, sizes),
        out_shape=(lam_type, sens_type, jax.ShapeDtypeStruct((ROWS, cols), f32)),
        in_specs=[in_hbm] * 3,
        out_specs=(in_vmem,) * 3,
        scratch_shapes=leaves,
        compiler_params=pltpu.CompilerParams(collective_id=0, has_side_effects=True, vmem_limit_bytes=limit),
        name="lattice",
    )(*[pltpu.with_memory_space_constraint(v, pltpu.HBM) for v in (populations, solid_fraction, labels)])
    scale = 1.0 / (STEPS * n_gz * n_gy * rows * cols)
    return pl.pallas_call(
        functools.partial(finish, scale),
        out_shape=(sens_type, lam_type),
        in_specs=[in_vmem] * 3,
        out_specs=(in_hbm,) * 2,
        scratch_shapes=[
            pltpu.VMEM(populations.shape, f32),
            pltpu.VMEM(solid_fraction.shape, f32),
            pltpu.VMEM((20 * rows * cols // LANES, 1, LANES), f32),
            pltpu.SemaphoreType.DMA((1,)),
        ],
        compiler_params=pltpu.CompilerParams(vmem_limit_bytes=4 * 1024 * 1024),
        name="finish",
    )(lam, sens, total)


def solution(mesh):
    n_gz, n_gy = mesh.shape["gz"], mesh.shape["gy"]
    n_core = 2
    n_z = 8 if n_gz % 16 == 0 else n_gz // 2
    n_x = n_gz // (n_core * n_z)
    in_specs = (P(None, "gz", "gy", None), P("gz", "gy", None), P("gz", "gy", None))
    out_specs = (P("gz", "gy", None), P(None, "gz", "gy", None))
    return jax.shard_map(
        functools.partial(on_device, (n_gz, n_gy, n_x, n_z, n_core)),
        mesh=mesh,
        in_specs=in_specs,
        out_specs=out_specs,
        check_vma=False,
    )
```

time: 34.4 us -> 31.3 us (0.910)
  the two profiles are of different devices: /device:TPU:8 before, /device:TPU:1 now
where the time goes in v4:
time: 31.3 us; the launch traced here: 31.2 us
  Pallas kernels  30.6 us (98%)
  between operations  0.64 us (2%)
    pallas_call x1, Pallas kernels, on_device(): pl.pallas_call(functools.partial(kernel, tree, sizes), out_shape=(lam_typ...  29.7 us
    pallas_call x1, Pallas kernels, on_device(): pl.pallas_call(functools.partial(finish, scale), out_shape=(sens_type, la...  0.84 us

profile of v4, /device:TPU:1, one launch (start us, length us, event | category | flops | bytes accessed | tf_op | source)
XLA Modules:
  0.0 31.2 jit_solution(1646081272889549875)
XLA Ops:
  0.6 29.7 %lattice.1 = (f32[19,1,32,256]{3,2,1,0:T(8,128)S(1)}, f32[1,32,256]{2,1,0:T(8,128)S(1)}, f32[8,256]{1,0:T(8,128)S(1)}) custom-call(f32[19,1,32,256]{3,2,1,0:T(8,128)} %pop_ref.1, f32[1,32,256]{2,1,0:T(8,128)} %sol_ref.1, s32[1,32,256]{2,1,0:T(8,128)} %lab_ref.1), custom_call_target="tpu_custom_call" | custom-call | tf_op jit(solution)/shard_map/lattice/pallas_call | solution.py:673
  30.4 0.8 %finish.1 = (f32[1,32,256]{2,1,0:T(8,128)}, f32[19,1,32,256]{3,2,1,0:T(8,128)}) custom-call(f32[19,1,32,256]{3,2,1,0:T(8,128)S(1)} %get-tuple-element.5.lam_ref, f32[1,32,256]{2,1,0:T(8,128)S(1)} %get-tuple-element.6.sens_ref, f32[8,256]{1,0:T(8,128)S(1)} %get-tuple-element.7.en_ref), custom_call_target="tpu_custom_call" | custom-call | tf_op jit(solution)/shard_map/finish/pallas_call | solution.py:683

commit v5 on v4

--- a/solution.py
+++ b/solution.py
@@ -77,27 +77,42 @@
     return signed([(c[i], vector[i]) for i in range(3)])
 
 
+def pair_moments(plus, minus, rest):
+    total = rest + functools.reduce(lambda p, q: p + q, list(plus.values()))
+    return total, [signed([(VEL[q][i], minus[q]) for q, o in PAIRS]) for i in range(3)]
+
+
 def collide(f, a, b, s, k):
-    rho = functools.reduce(lambda p, q: p + q, f)
-    m = [signed([(VEL[q][i], f[q]) for q in range(19)]) for i in range(3)]
+    plus = {q: f[q] + f[o] for q, o in PAIRS}
+    minus = {q: f[q] - f[o] for q, o in PAIRS}
+    rho, m = pair_moments(plus, minus, f[0])
     inv = 1.0 / rho
     u = [m[i] * inv for i in range(3)]
     speed = u[0] * u[0] + u[1] * u[1] + u[2] * u[2]
     brho = b * rho
     base = brho * (1.0 - 1.5 * speed)
+    both, half_sum, half_diff = a + s, 0.5 * (a + s), 0.5 * (a - s)
+    bases = {w: w * base for w in set(WEIGHT)}
+    level = {w: bases[w] + k * inlet_value(q) for w, q in ((WEIGHT[0], 0), (WEIGHT[1], 1), (WEIGHT[7], 7))}
     post = [None] * 19
-    post[0] = (a + s) * f[0] + WEIGHT[0] * base + k * inlet_value(0)
+    post[0] = both * f[0] + level[WEIGHT[0]]
     for q, o in PAIRS:
         w = WEIGHT[q]
         along = dot_c(VEL[q], u)
-        even = w * base + (4.5 * w) * (brho * along) * along
-        odd = (3.0 * w) * (brho * along)
-        post[q] = a * f[q] + s * f[o] + (even + odd) + k * inlet_value(q)
-        post[o] = a * f[o] + s * f[q] + (even - odd) + k * inlet_value(o)
+        flow = brho * along
+        even = half_sum * plus[q] + (4.5 * w) * (flow * along)
+        odd = half_diff * minus[q] + (3.0 * w) * flow
+        if VEL[q][2] == 0:
+            even = even + level[w]
+        else:
+            even = even + (bases[w] + k * (0.5 * (inlet_value(q) + inlet_value(o))))
+            odd = odd + k * (0.5 * (inlet_value(q) - inlet_value(o)))
+        post[q] = even + odd
+        post[o] = even - odd
     return rho, u, speed, post
 
 
-def collide_adjoint(mu, f, rho, u, speed, a, b, s):
+def collide_adjoint(mu, f, rho, u, speed, a, b, s, extra=None):
     plus = {q: mu[q] + mu[o] for q, o in PAIRS}
     minus = {q: mu[q] - mu[o] for q, o in PAIRS}
 
@@ -119,22 +134,30 @@
     for i in range(3):
         for j in range(i, 3):
             big_c[i, j] = big_c[j, i] = 4.5 * weighted(plus, i, j)
-    cu = [sum(big_c[i, j] * u[j] for j in range(3)) for i in range(3)]
+    cu = [big_c[i, 0] * u[0] + big_c[i, 1] * u[1] + big_c[i, 2] * u[2] for i in range(3)]
     quad = cu[0] * u[0] + cu[1] * u[1] + cu[2] * u[2] - 1.5 * speed * big_a
     by_rho = b * (big_a - quad)
-    by_m = [b * (big_b[i] + 2.0 * cu[i] - 3.0 * big_a * u[i]) for i in range(3)]
+    triple = 3.0 * big_a
+    by_m = [b * (big_b[i] + 2.0 * cu[i] - triple * u[i]) for i in range(3)]
+    if extra is not None:
+        by_rho = by_rho + extra[0]
+        by_m = [by_m[i] + extra[1][i] for i in range(3)]
+    both, half_sum, half_diff = a + s, 0.5 * (a + s), 0.5 * (a - s)
     lam = [None] * 19
-    lam[0] = (a + s) * mu[0] + by_rho
-    same = mu[0] * f[0]
-    cross = same
+    lam[0] = both * mu[0] + by_rho
+    sums, differences = [], []
     for q, o in PAIRS:
-        along = dot_c(VEL[q], by_m)
-        lam[q] = a * mu[q] + s * mu[o] + (by_rho + along)
-        lam[o] = a * mu[o] + s * mu[q] + (by_rho - along)
-        same = same + (mu[q] * f[q] + mu[o] * f[o])
-        cross = cross + (mu[q] * f[o] + mu[o] * f[q])
+        even = half_sum * plus[q] + by_rho
+        odd = half_diff * minus[q] + dot_c(VEL[q], by_m)
+        lam[q] = even + odd
+        lam[o] = even - odd
+        sums.append(plus[q] * (f[q] + f[o]))
+        differences.append(minus[q] * (f[q] - f[o]))
+    all_sums = functools.reduce(lambda p, q: p + q, sums)
+    all_differences = functools.reduce(lambda p, q: p + q, differences)
+    middle = mu[0] * f[0]
     total = rho * (big_a + big_b[0] * u[0] + big_b[1] * u[1] + big_b[2] * u[2] + quad)
-    by_s = cross - ((1.0 - OMEGA) * same + OMEGA * total)
+    by_s = OMEGA * (middle + 0.5 * all_sums - total) - (1.0 - 0.5 * OMEGA) * all_differences
     return lam, by_s
 
 
@@ -179,10 +202,8 @@
         yd={r: vmem(n, cols) for r, n in EDGE_ROWS},
         ryu={r: vmem(n, cols) for r, n in EDGE_ROWS},
         ryd={r: vmem(n, cols) for r, n in EDGE_ROWS},
-        up={r: vmem(5, rows, cols) for r in (0, 3)},
-        dn={r: vmem(5, rows, cols) for r in (0, 3)},
-        rup={r: vmem(5, padded, cols) for r in (0, 3)},
-        rdn={r: vmem(5, padded, cols) for r in (0, 3)},
+        out={r: vmem(2, 5, rows, cols) for r in (0, 3)},
+        arrived={r: vmem(2, 5, padded, cols) for r in (0, 3)},
         flat={r: vmem(9, padded, cols) for r in (0, 3)},
         dg=[[vmem(1, cols) for i in range(4)] for r in range(4)],
         rdg=[[vmem(1, cols) for i in range(4)] for r in range(4)],
@@ -196,7 +217,7 @@
     n_gz, n_gy, n_x, n_z, n_core = sizes
     rows, cols = S.ds.shape
     chunks = rows // ROWS
-    order = [0, chunks - 1, *range(1, chunks - 1)]
+    order = [chunks - 1, 0, *range(chunks - 2, 0, -1)]
     last = TOP + rows
     gz = lax.axis_index("gz")
     gy = lax.axis_index("gy")
@@ -269,30 +290,33 @@
     def send_bulk(r, k):
         src, dst = pl.ds(k * ROWS, ROWS), pl.ds(TOP + k * ROWS, ROWS)
         if r in (0, 3):
-            send(S.up[r].at[:, src, :], S.rup[r].at[:, dst, :], r, k, at(1, 0))
-            send(S.dn[r].at[:, src, :], S.rdn[r].at[:, dst, :], r, chunks + k, at(-1, 0))
+            send(S.out[r].at[0, :, src, :], S.arrived[r].at[0, :, dst, :], r, k, at(far, 0))
+            send(S.out[r].at[1, :, src, :], S.arrived[r].at[1, :, dst, :], r, chunks + k, at(near_z, 0))
         if r == 1:
+            send(S.out1.at[0, :, dst, :], S.in1.at[0, :, dst, :], 1, k, at(far, 0))
             send(S.out1.at[1, :, dst, :], S.in1.at[1, :, dst, :], 1, chunks + k, at(near_z, 0))
-            send(S.out1.at[0, :, dst, :], S.in1.at[0, :, dst, :], 1, k, at(far, 0))
         if r == 2:
             send(S.mine.at[:, src, :], S.side.at[1, :, dst, :], 2, chunks + k, at(near_z, 0))
         if r == 4:
             send(S.rest.at[:, src, :], S.far_rest.at[:, src, :], 4, k, at(far, 0))
 
-    def send_edges(r):
+    def send_edges(r, end):
+        high = end == 1
         if r == 4:
-            send(S.rest_hi, S.far_rest_hi, 4, base + 2, at(far, 1))
-            send(S.rest_lo, S.far_rest_lo, 4, base + 3, at(far, -1))
+            src, dst = (S.rest_hi, S.far_rest_hi) if high else (S.rest_lo, S.far_rest_lo)
+            send(src, dst, 4, base + (2 if high else 3), at(far, end))
             return
-        send(S.yu[r], S.ryu[r], r, base, at(0, 1))
-        send(S.yd[r], S.ryd[r], r, base + 1, at(0, -1))
+        src, dst = (S.yu, S.ryu) if high else (S.yd, S.ryd)
+        send(src[r], dst[r], r, base + (0 if high else 1), at(0, end))
         for i, (dz, dy) in enumerate(DIAGONAL if r in (0, 3) else FAR_DIAGONAL):
-            if r != 2 or i >= 2:
+            if dy == end and (r != 2 or i >= 2):
                 send(S.dg[r][i], S.rdg[r][i], r, base + 2 + i, at(dz, dy))
 
     def send_chunk(r, k):
         if k == chunks - 1:
-            send_edges(r)
+            send_edges(r, 1)
+        if k == 0:
+            send_edges(r, -1)
         send_bulk(r, k)
 
     def sent(*rounds):
@@ -321,11 +345,11 @@
 
     def emit_populations(r, k, values, sense):
         here = pl.ds(k * ROWS, ROWS)
-        for moving, table in ((S.up, UP), (S.dn, DOWN)):
+        for side, table in ((upward, UP), (downward, DOWN)):
             for i, d in enumerate(table):
                 q = INDEX[tuple(sense * e for e in d)]
                 value = roll_x(values[q], d[0])
-                moving[r][i, here, :] = value
+                S.out[r][side, i, here, :] = value
                 slot = DIAGONAL.index((d[2], d[1])) if d[1] else None
                 if d[1] == 1 and k == chunks - 1:
                     S.dg[r][slot][...] = value[ROWS - 1 :, :]
@@ -343,19 +367,20 @@
                 S.yd[r][j : j + 1, :] = value[:1, :]
 
     def place_edges(r):
-        for i, arrived, row in ((0, S.rup, TOP - 1), (1, S.rup, last), (2, S.rdn, TOP - 1), (3, S.rdn, last)):
+        for i, side, row in ((0, downward, TOP - 1), (1, downward, last), (2, upward, TOP - 1), (3, upward, last)):
             slot = 3 if i % 2 == 0 else 4
-            arrived[r][slot, pl.ds(row, 1), :] = S.rdg[r][i][...]
+            S.arrived[r][side, slot, pl.ds(row, 1), :] = S.rdg[r][i][...]
         for j in range(3):
             S.flat[r][FLAT.index(FLAT_UP[j]), pl.ds(TOP - 1, 1), :] = S.ryu[r][j : j + 1, :]
             S.flat[r][FLAT.index(FLAT_DOWN[j]), pl.ds(last, 1), :] = S.ryd[r][j : j + 1, :]
 
     def gather_populations(r, k, sense):
         values = [None] * 19
-        for arrived, table in ((S.rup, UP), (S.rdn, DOWN), (S.flat, FLAT)):
+        for i, d in enumerate(FLAT):
+            values[INDEX[tuple(sense * e for e in d)]] = S.flat[r][i, moved(k, d[1]), :]
+        for side, table in ((downward, UP), (upward, DOWN)):
             for i, d in enumerate(table):
-                q = INDEX[tuple(sense * e for e in d)]
-                values[q] = arrived[r][i, moved(k, d[1]), :]
+                values[INDEX[tuple(sense * e for e in d)]] = S.arrived[r][side, i, moved(k, d[1]), :]
         return values
 
     def coefficients(k):
@@ -382,7 +407,8 @@
         emit_populations(0, k, post, 1)
 
     pl.semaphore_wait(barrier, len(greeted))
-    send_edges(0)
+    send_edges(0, 1)
+    send_edges(0, -1)
     for k in order:
         send_bulk(0, k)
     S.s_hi[...] = S.coef[2, pl.ds(rows - 1, 1), :]
@@ -405,7 +431,7 @@
         flow = rho * speed
         S.ds[here, :] = -flow
         energy = (1.0 - s) * flow
-        S.acc[...] = energy if k == 0 else S.acc[...] + energy
+        S.acc[...] = energy if k == order[0] else S.acc[...] + energy
 
         def three(cy, cz):
             mid = post[INDEX[0, cy, cz]]
@@ -612,16 +638,11 @@
         f = [S.f1[q, here, :] for q in range(19)]
         rho, u = S.mom1[0, here, :], [S.mom1[i, here, :] for i in (1, 2, 3)]
         speed = u[0] * u[0] + u[1] * u[1] + u[2] * u[2]
-        lam, by_s = collide_adjoint(mu, f, rho, u, speed, a, b, s)
+        free = 1.0 - s
+        twice = 2.0 * free
+        extra = (-(free * speed), [twice * u[i] for i in range(3)])
+        lam, by_s = collide_adjoint(mu, f, rho, u, speed, a, b, s, extra)
         S.ds[here, :] = S.ds[here, :] + by_s
-        twice = 2.0 * (1.0 - s)
-        twice_u = [twice * u[i] for i in range(3)]
-        e = (1.0 - s) * speed
-        lam[0] = lam[0] - e
-        for q, o in PAIRS:
-            along = dot_c(VEL[q], twice_u)
-            lam[q] = lam[q] + (along - e)
-            lam[o] = lam[o] - (along + e)
         emit_populations(3, k, lam, -1)
         send_chunk(3, k)
 

time: 31.3 us -> 30.9 us (0.987)
  Pallas kernels: 30.6 us -> 30.2 us
    pallas_call x1, Pallas kernels: 29.7 us -> 29.4 us  [on_device(): pl.pallas_call(functools.partial(kernel, tree, sizes), out_shape=(lam_typ...]
where the time goes in v5:
time: 30.9 us; the launch traced here: 30.8 us
  Pallas kernels  30.2 us (98%)
  between operations  0.64 us (2%)
    pallas_call x1, Pallas kernels, on_device(): pl.pallas_call(functools.partial(kernel, tree, sizes), out_shape=(lam_typ...  29.4 us
    pallas_call x1, Pallas kernels, on_device(): pl.pallas_call(functools.partial(finish, scale), out_shape=(sens_type, la...  0.84 us

profile of v5, /device:TPU:1, one launch (start us, length us, event | category | flops | bytes accessed | tf_op | source)
XLA Modules:
  0.0 30.8 jit_solution(17074672229545273212)
XLA Ops:
  0.6 29.4 %lattice.1 = (f32[19,1,32,256]{3,2,1,0:T(8,128)S(1)}, f32[1,32,256]{2,1,0:T(8,128)S(1)}, f32[8,256]{1,0:T(8,128)S(1)}) custom-call(f32[19,1,32,256]{3,2,1,0:T(8,128)} %pop_ref.1, f32[1,32,256]{2,1,0:T(8,128)} %sol_ref.1, s32[1,32,256]{2,1,0:T(8,128)} %lab_ref.1), custom_call_target="tpu_custom_call" | custom-call | tf_op jit(solution)/shard_map/lattice/pallas_call | solution.py:694
  30.0 0.8 %finish.1 = (f32[1,32,256]{2,1,0:T(8,128)}, f32[19,1,32,256]{3,2,1,0:T(8,128)}) custom-call(f32[19,1,32,256]{3,2,1,0:T(8,128)S(1)} %get-tuple-element.5.lam_ref, f32[1,32,256]{2,1,0:T(8,128)S(1)} %get-tuple-element.6.sens_ref, f32[8,256]{1,0:T(8,128)S(1)} %get-tuple-element.7.en_ref), custom_call_target="tpu_custom_call" | custom-call | tf_op jit(solution)/shard_map/finish/pallas_call | solution.py:704

commit v6 on v5

--- a/solution.py
+++ b/solution.py
@@ -218,6 +218,7 @@
     rows, cols = S.ds.shape
     chunks = rows // ROWS
     order = [chunks - 1, 0, *range(chunks - 2, 0, -1)]
+    late_order = [*range(1, chunks - 1), chunks - 1, 0]
     last = TOP + rows
     gz = lax.axis_index("gz")
     gy = lax.axis_index("gy")
@@ -263,6 +264,8 @@
             name = "E"
         else:
             name = "B" if i % chunks == order[-1] and r != 5 else "A"
+        if r == 4 and i < base:
+            name = "B" if i in (0, chunks - 1) else "A"
         if r == 1:
             near_side = i - base not in (2, 3) if i >= base else i >= chunks
             name = ("n" if near_side else "f") + name
@@ -330,12 +333,20 @@
             landed.add((r, name))
             wait_bytes(group_bytes[r, name], S.rsem.at[GROUPS.index((r, name))])
 
-    def receive(r, k, side="", reach=1):
+    def receive(r, k, side=""):
         receive_group(r, side + "A")
-        if abs(k - order[-1]) <= reach:
+        if abs(k - order[-1]) <= 1:
             receive_group(r, side + "B")
         receive_group(r, side + "E")
         return k == order[0]
+
+    def receive_late(r, k, side=""):
+        receive_group(r, side + "A")
+        receive_group(r, side + "B")
+        first = k == late_order[-2]
+        if first:
+            receive_group(r, side + "E")
+        return first
 
     def interior(k):
         return pl.ds(TOP + k * ROWS, ROWS)
@@ -473,9 +484,9 @@
         S.in1[side, 2, pl.ds(TOP - 1, 1), :] = S.rdg[1][i][...]
         S.in1[side, 3, pl.ds(last, 1), :] = S.rdg[1][i + 1][...]
 
-    for k in order:
-        here = pl.ds(k * ROWS, ROWS)
-        if receive(1, k, "n"):
+    for k in late_order:
+        here = pl.ds(k * ROWS, ROWS)
+        if receive_late(1, k, "n"):
             place_halo(1, 2)
             for j in range(2):
                 S.part[2 + j, pl.ds(TOP - 1, 1), :] = S.ryu[1][j : j + 1, :]
@@ -574,10 +585,13 @@
         rho, speed, (x, y, z), free = finish_moments(rest, total, along, ahead, behind, s)
         return x, y, z - free * speed
 
-    for k in order:
+    for k in late_order:
         here = pl.ds(k * ROWS, ROWS)
         receive_group(5, "A")
-        if receive(4, k, "", 0):
+        receive_group(4, "A")
+        if k == late_order[-2]:
+            receive_group(4, "B")
+            receive_group(4, "E")
             low, high = pl.ds(TOP - 1, 1), pl.ds(last, 1)
             x, y, w = far_plane(
                 [S.far_rest_hi[i : i + 1, :] for i in range(4)],
@@ -649,9 +663,9 @@
     reduce_send(1, reduce_receive(0))
     sent(4, 2, 3, 6, 7)
 
-    for k in order:
-        here = pl.ds(k * ROWS, ROWS)
-        if receive(3, k):
+    for k in late_order:
+        here = pl.ds(k * ROWS, ROWS)
+        if receive_late(3, k):
             place_edges(3)
         a, b, s = coefficients(k)
         mu = gather_populations(3, k, -1)

time: 30.9 us -> 30.7 us (level)
  no operation moved by 1% of the time
where the time goes in v6:
time: 30.7 us; the launch traced here: 30.6 us
  Pallas kernels  29.9 us (97%)
  between operations  0.64 us (2%)
    pallas_call x1, Pallas kernels, on_device(): pl.pallas_call(functools.partial(kernel, tree, sizes), out_shape=(lam_typ...  29.1 us
    pallas_call x1, Pallas kernels, on_device(): pl.pallas_call(functools.partial(finish, scale), out_shape=(sens_type, la...  0.84 us

profile of v6, /device:TPU:1, one launch (start us, length us, event | category | flops | bytes accessed | tf_op | source)
XLA Modules:
  0.0 30.6 jit_solution(7247289172938369107)
XLA Ops:
  0.6 29.1 %lattice.1 = (f32[19,1,32,256]{3,2,1,0:T(8,128)S(1)}, f32[1,32,256]{2,1,0:T(8,128)S(1)}, f32[8,256]{1,0:T(8,128)S(1)}) custom-call(f32[19,1,32,256]{3,2,1,0:T(8,128)} %pop_ref.1, f32[1,32,256]{2,1,0:T(8,128)} %sol_ref.1, s32[1,32,256]{2,1,0:T(8,128)} %lab_ref.1), custom_call_target="tpu_custom_call" | custom-call | tf_op jit(solution)/shard_map/lattice/pallas_call | solution.py:708
  29.8 0.8 %finish.1 = (f32[1,32,256]{2,1,0:T(8,128)}, f32[19,1,32,256]{3,2,1,0:T(8,128)}) custom-call(f32[19,1,32,256]{3,2,1,0:T(8,128)S(1)} %get-tuple-element.5.lam_ref, f32[1,32,256]{2,1,0:T(8,128)S(1)} %get-tuple-element.6.sens_ref, f32[8,256]{1,0:T(8,128)S(1)} %get-tuple-element.7.en_ref), custom_call_target="tpu_custom_call" | custom-call | tf_op jit(solution)/shard_map/finish/pallas_call | solution.py:718

commit v7 on v6

--- a/solution.py
+++ b/solution.py
@@ -523,9 +523,9 @@
         twice = 2.0 * free
         return rho, speed, [twice * v for v in u], free
 
-    for k in order:
-        here = pl.ds(k * ROWS, ROWS)
-        if receive(1, k, "f"):
+    for k in late_order:
+        here = pl.ds(k * ROWS, ROWS)
+        if receive_late(1, k, "f"):
             place_halo(0, 0)
         rho, speed, (x, y, z), free = finish_moments(
             [S.rest[i, here, :] for i in range(4)],

time: 30.7 us -> 30.8 us (level)
  no operation moved by 1% of the time
where the time goes in v7:
time: 30.8 us; the launch traced here: 30.7 us
  Pallas kernels  30 us (97%)
  between operations  0.64 us (2%)
    pallas_call x1, Pallas kernels, on_device(): pl.pallas_call(functools.partial(kernel, tree, sizes), out_shape=(lam_typ...  29.2 us
    pallas_call x1, Pallas kernels, on_device(): pl.pallas_call(functools.partial(finish, scale), out_shape=(sens_type, la...  0.84 us

profile of v7, /device:TPU:1, one launch (start us, length us, event | category | flops | bytes accessed | tf_op | source)
XLA Modules:
  0.0 30.7 jit_solution(14220534934076000164)
XLA Ops:
  0.6 29.2 %lattice.1 = (f32[19,1,32,256]{3,2,1,0:T(8,128)S(1)}, f32[1,32,256]{2,1,0:T(8,128)S(1)}, f32[8,256]{1,0:T(8,128)S(1)}) custom-call(f32[19,1,32,256]{3,2,1,0:T(8,128)} %pop_ref.1, f32[1,32,256]{2,1,0:T(8,128)} %sol_ref.1, s32[1,32,256]{2,1,0:T(8,128)} %lab_ref.1), custom_call_target="tpu_custom_call" | custom-call | tf_op jit(solution)/shard_map/lattice/pallas_call | solution.py:708
  29.8 0.8 %finish.1 = (f32[1,32,256]{2,1,0:T(8,128)}, f32[19,1,32,256]{3,2,1,0:T(8,128)}) custom-call(f32[19,1,32,256]{3,2,1,0:T(8,128)S(1)} %get-tuple-element.5.lam_ref, f32[1,32,256]{2,1,0:T(8,128)S(1)} %get-tuple-element.6.sens_ref, f32[8,256]{1,0:T(8,128)S(1)} %get-tuple-element.7.en_ref), custom_call_target="tpu_custom_call" | custom-call | tf_op jit(solution)/shard_map/finish/pallas_call | solution.py:718

commit v8 on v7

--- a/solution.py
+++ b/solution.py
@@ -230,10 +230,6 @@
         some = S.some.at[pl.ds(0, count)]
         pltpu.make_async_copy(some, some, sem).wait()
 
-    loads = ((pop_ref, S.f0), (sol_ref, S.sol), (lab_ref, S.lab))
-    for src, dst in loads:
-        pltpu.make_async_copy(src, dst, S.in_sem.at[0]).start()
-
     def at(dz, dy):
         return (lax.rem(gz + dz + n_gz, n_gz), lax.rem(gy + dy + n_gy, n_gy))
 
@@ -256,6 +252,10 @@
     greeted = near + stages[0] + [place(dx, 0, 0, 0) for dx in range(1, n_x)]
     for device in greeted:
         pl.semaphore_signal(barrier, inc=1, device_id=device, device_id_type=MESH)
+
+    loads = ((pop_ref, S.f0), (sol_ref, S.sol), (lab_ref, S.lab))
+    for src, dst in loads:
+        pltpu.make_async_copy(src, dst, S.in_sem.at[0]).start()
 
     sent_bytes, group_bytes = {}, {}
 

time: 30.8 us -> 30.8 us (level)
  no operation moved by 1% of the time
where the time goes in v8:
time: 30.8 us; the launch traced here: 30.7 us
  Pallas kernels  30 us (97%)
  between operations  0.64 us (2%)
    pallas_call x1, Pallas kernels, on_device(): pl.pallas_call(functools.partial(kernel, tree, sizes), out_shape=(lam_typ...  29.2 us
    pallas_call x1, Pallas kernels, on_device(): pl.pallas_call(functools.partial(finish, scale), out_shape=(sens_type, la...  0.84 us

profile of v8, /device:TPU:1, one launch (start us, length us, event | category | flops | bytes accessed | tf_op | source)
XLA Modules:
  0.0 30.7 jit_solution(2326914712123398977)
XLA Ops:
  0.6 29.2 %lattice.1 = (f32[19,1,32,256]{3,2,1,0:T(8,128)S(1)}, f32[1,32,256]{2,1,0:T(8,128)S(1)}, f32[8,256]{1,0:T(8,128)S(1)}) custom-call(f32[19,1,32,256]{3,2,1,0:T(8,128)} %pop_ref.1, f32[1,32,256]{2,1,0:T(8,128)} %sol_ref.1, s32[1,32,256]{2,1,0:T(8,128)} %lab_ref.1), custom_call_target="tpu_custom_call" | custom-call | tf_op jit(solution)/shard_map/lattice/pallas_call | solution.py:708
  29.8 0.8 %finish.1 = (f32[1,32,256]{2,1,0:T(8,128)}, f32[19,1,32,256]{3,2,1,0:T(8,128)}) custom-call(f32[19,1,32,256]{3,2,1,0:T(8,128)S(1)} %get-tuple-element.5.lam_ref, f32[1,32,256]{2,1,0:T(8,128)S(1)} %get-tuple-element.6.sens_ref, f32[8,256]{1,0:T(8,128)S(1)} %get-tuple-element.7.en_ref), custom_call_target="tpu_custom_call" | custom-call | tf_op jit(solution)/shard_map/finish/pallas_call | solution.py:718
